TPU v7x, 32 devices: a whole 2x2x4 slice. The times are simulated.
32 devices in a mesh: groups: 2 (over x), seq: 16 (over z, y, core).
Axes of the slice: x: 2, y: 2, z: 4, core: 2. Of those that a mesh axis runs over, the one named last changes fastest.
Arguments:
- queries: bfloat16 [96, 8192], P(('groups', 'seq')), parts along dimension 0, may hold values from -48 to 48
- prompt_of: int32 [96, 1], P(('groups', 'seq')), parts along dimension 0, may hold values from 0 to 1; in each aligned block of 3 rows (0 to 2, 3 to 5, ...) at most 2 rows name the same one
- suffix_cache: bfloat16 [96, 512, 2048], P(('groups', 'seq')), parts along dimension 0, may hold values from -6 to 6
- suffix_blocks: int32 [96], P(('groups', 'seq')), parts along dimension 0, may hold values from 1 to 4
- prompt_cache: bfloat16 [4, 2048, 2048], P('groups', 'seq'), parts along dimension 0, may hold values from -16 to 16
- reward_weight: float32 [8192], replicated, may hold values from -0.4375 to 0.4375
Outputs:
- attended: bfloat16 [96, 8192], P(('groups', 'seq')), parts along dimension 0
- scores: float32 [96], P(('groups', 'seq')), parts along dimension 0
There are 2 independent parts, one for each index of `groups`. A program takes and returns all parts, laid end to end along the dimension named above; an argument that names none is the same for every part. Nothing has to cross between parts.
Inputs may be any that keep to these rules, and one draw needn't show every extreme that they name: `prompt_of`: in each device's aligned block of 3 rows at most 2 candidates name the same prompt.
All inputs are finite; a program needn't handle non-finite values.
Results may differ from a plain program's by a relative error of at most 0.015.
Values may be sent and summed in bfloat16 or wider, within the bound.
No kernel may reach another device: no remote copies, remote signals or barrier semaphores. Data moves between devices by JAX's collectives and lax.ppermute only.
A program may use at most 192 MiB of HBM per device.

v0:
```python
import math

import jax
import jax.numpy as jnp
from jax import lax
from jax.sharding import PartitionSpec as P

HD = 128
CAP = 2
BLOCK = 128


floor_logit = -1e30


def attend_block(query_rows, keys, values):
    row_count = query_rows.shape[0]
    kv_heads = keys.shape[1]
    head_dim = keys.shape[2]
    grouped = query_rows.reshape(row_count, kv_heads, -1, head_dim)
    logits = jnp.einsum(
        "nkgd,tkd->nkgt", grouped, keys, preferred_element_type=jnp.float32
    ) * head_dim ** (-0.5)
    maxima = jnp.max(logits, axis=-1)
    exponent = jnp.exp(logits - maxima[..., None])
    totals = jnp.sum(exponent, axis=-1)
    weights = exponent.astype(jnp.bfloat16)
    weighted = jnp.einsum("nkgt,tkd->nkgd", weights, values, preferred_element_type=jnp.float32)
    return (
        maxima.reshape(row_count, -1),
        totals.reshape(row_count, -1),
        weighted.reshape(row_count, -1),
    )


def body(queries, prompt_of, suffix_cache, suffix_blocks, prompt_cache, reward_weight):
    cand_rows = queries.shape[0]
    prompts = prompt_cache.shape[0]
    prompt_span = prompt_cache.shape[1]
    kv_width = prompt_cache.shape[2] // 2
    kv_heads = kv_width // HD
    heads = queries.shape[1] // HD
    keys_local = prompt_cache[:, :, :kv_width].reshape(prompts, prompt_span, kv_heads, HD)
    values_local = prompt_cache[:, :, kv_width:].reshape(prompts, prompt_span, kv_heads, HD)
    suffix_len = suffix_cache.shape[1]
    suffix_keys = suffix_cache[:, :, :kv_width].reshape(cand_rows, suffix_len, kv_heads, HD)
    suffix_values = suffix_cache[:, :, kv_width:].reshape(cand_rows, suffix_len, kv_heads, HD)
    grouped = queries.reshape(cand_rows, kv_heads, -1, HD)
    logits = jnp.einsum(
        "ckgd,ctkd->ckgt", grouped, suffix_keys, preferred_element_type=jnp.float32
    ) * HD ** (-0.5)
    live_mask = (jnp.arange(suffix_len)[None, :] < BLOCK * suffix_blocks[:, None])[:, None, None, :]
    logits = jnp.where(live_mask, logits, floor_logit)
    maxima = jnp.max(logits, axis=-1)
    exponent = jnp.where(live_mask, jnp.exp(logits - maxima[..., None]), 0.0)
    totals = jnp.sum(exponent, axis=-1)
    weighted = jnp.einsum(
        "ckgt,ctkd->ckgd",
        exponent.astype(jnp.bfloat16),
        suffix_values,
        preferred_element_type=jnp.float32,
    )
    suffix_state = (
        maxima.reshape(cand_rows, -1),
        totals.reshape(cand_rows, -1),
        weighted.reshape(cand_rows, -1),
    )
    prompt_ids = prompt_of[:, 0]
    prompt_hot = (prompt_ids[:, None] == jnp.arange(prompts)[None, :]).astype(jnp.float32)
    spread = 1
    earlier = (jnp.arange(cand_rows)[:, None] > jnp.arange(cand_rows)[None, :]).astype(jnp.float32)
    slot_rank = jnp.sum(jnp.dot(earlier, prompt_hot) * prompt_hot, axis=1).astype(jnp.int32)
    slot_index = prompt_ids * CAP + slot_rank
    slot_hot = (slot_index[:, None] == jnp.arange(prompts * CAP)[None, :]).astype(jnp.float32)
    row_block = jnp.einsum(
        "cs,cf->sf", slot_hot.astype(jnp.bfloat16), queries, preferred_element_type=jnp.float32
    ).astype(jnp.bfloat16)
    home_state = tuple(
        (
            jnp.einsum("cs,cf->sf", slot_hot, member, precision=lax.Precision.HIGHEST)
            for member in suffix_state
        )
    )

    def attend_rows(query_rows):
        shards = query_rows.shape[0] // (prompts * CAP)
        shaped = query_rows.reshape(shards, prompts, CAP, -1)
        parts_all = [
            attend_block(
                shaped[:, prompt].reshape(shards * CAP, -1),
                keys_local[prompt],
                values_local[prompt],
            )
            for prompt in range(prompts)
        ]
        return tuple(
            (
                jnp.stack(
                    [
                        parts_all[prompt][member].reshape(shards, CAP, -1)
                        for prompt in range(prompts)
                    ],
                    axis=1,
                ).reshape(shards * prompts * CAP, -1)
                for member in range(3)
            )
        )

    rows_dev = row_block.shape[0]
    width_heads = heads * spread
    devices = lax.axis_size("seq")
    query_rows = (lax.all_gather(row_block, "seq", axis=0, tiled=True),)[0]
    shards = query_rows.shape[0] // rows_dev
    block_size = math.gcd(shards, 16)
    query_blocks = query_rows.reshape(shards // block_size, block_size * rows_dev, -1)
    mapped = lax.map(attend_rows, query_blocks)
    fresh_state = tuple((member.reshape(shards * rows_dev, -1) for member in mapped))
    computed = tuple((fresh_rows for fresh_rows in fresh_state))
    returned = (
        lax.all_to_all(computed[0], "seq", split_axis=0, concat_axis=0, tiled=True),
        lax.all_to_all(computed[1], "seq", split_axis=0, concat_axis=0, tiled=True),
        lax.all_to_all(computed[2], "seq", split_axis=0, concat_axis=0, tiled=True),
    )
    back_max = returned[0].reshape(devices, rows_dev, width_heads)
    back_sum = returned[1].reshape(devices, rows_dev, width_heads)
    back_mix = returned[2].reshape(devices, rows_dev, width_heads, HD)
    joined = jnp.maximum(jnp.max(back_max, axis=0), home_state[0])
    factor = jnp.exp(back_max - joined[None])
    home_factor = jnp.exp(home_state[0] - joined)
    totals_all = jnp.sum(factor * back_sum, axis=0) + home_factor * home_state[1]
    mixed_all = jnp.sum(factor[..., None] * back_mix, axis=0) + home_factor[..., None] * home_state[
        2
    ].reshape(rows_dev, width_heads, HD)
    final_state = (joined, totals_all, mixed_all.reshape(rows_dev, -1))
    out_rows = final_state[1].shape[0]
    attended_rows = (
        final_state[2].reshape(out_rows, heads, HD) / final_state[1][..., None]
    ).reshape(out_rows, -1)
    attended = jnp.einsum(
        "cs,sf->cf", slot_hot, attended_rows, precision=lax.Precision.HIGHEST
    ).astype(jnp.bfloat16)
    scores = jnp.sum(attended.astype(jnp.float32) * reward_weight, axis=-1)
    return (attended, scores)


def solution(mesh):
    placed = (
        P(("groups", "seq"), None),
        P(("groups", "seq"), None),
        P(("groups", "seq"), None, None),
        P(("groups", "seq")),
        P("groups", "seq", None),
        P(),
    )
    return jax.shard_map(
        body,
        mesh=mesh,
        in_specs=placed,
        out_specs=(P(("groups", "seq"), None), P(("groups", "seq"))),
        check_vma=False,
    )
```

profile of v0, /device:TPU:13, one launch (start us, length us, event | category | flops | bytes accessed | tf_op | source)
XLA Modules:
  0.0 144.2 jit_solution(13109195820663340520)
XLA Ops:
  7.2 0.9 fusion.8
  8.1 0.7 fusion.38
  8.7 0.5 copy-done.5
  9.2 1.6 %fusion = bf16[1,4,8192]{2,1,0:T(4,128)(2,1)} fusion(bf16[3,8192]{1,0:T(4,128)(2,1)} %param.6, s32[3]{0:T(128)S(1)} %fusion.38), kind=kOutput, calls=%fused_computation.2 | convolution fusion | flops 229412 | bytes 114700 | tf_op jit(solution)/shard_map/cs,cf->sf/dot_general | solution.py:75
  10.9 1.3 fusion.42
  12.1 0.2 copy.104
  12.3 0.2 copy.102
  12.5 0.9 copy.107
  13.4 0.9 copy.106
  14.2 34.8 %all-gather.3.cloned.1.call-done = bf16[16,4,8192]{2,1,0:T(4,128)(2,1)} async-done(((bf16[1,4,8192]{2,1,0:T(4,128)(2,1)}), bf16[16,4,8192]{2,1,0:T(4,128)(2,1)}) %all-gather.3.cloned.1.call-update) | async-done | bytes 1048592 | tf_op jit(solution)/shard_map/all_gather | solution.py:112
  49.0 2.8 %reshape.139 = bf16[16,2,2,8192]{3,2,1,0:T(2,128)(2,1)S(1)} reshape(bf16[16,4,8192]{2,1,0:T(4,128)(2,1)} %all-gather.3.cloned.1.call-done) | data formatting | bytes 2097152 | tf_op jit(solution)/shard_map/while/body/eval_jaxpr/reshape | solution.py:87
  51.8 1.2 slice_bitcast_fusion.1
  53.0 0.4 squeeze.30
  53.4 0.5 fusion.44
  54.0 0.1 copy.66
  54.0 0.7 fusion.11
  54.7 0.1 copy.83
  54.8 0.1 reshape.150
  54.9 0.4 squeeze.28
  55.3 0.5 fusion.45
  55.8 0.1 copy.61
  55.9 0.7 fusion.9
  56.5 0.1 copy.82
  56.6 0.1 reshape.149
  56.8 0.7 reshape.163
  57.5 5.4 %all-to-all-start.2 = ((f32[16,1,256]{2,1,0:T(1,128)}), f32[16,1,256]{2,1,0:T(1,128)S(1)}, u32[]{:S(2)}, u32[]{:S(2)}) async-start(f32[16,1,256]{2,1,0:T(1,128)} %reshape.163), calls=%async_computation.2 | async-start | bytes 32768 | tf_op jit(solution)/shard_map/all_to_all | solution.py:121
  62.9 0.1 reshape.141
  63.0 0.1 reshape.140
  63.1 1.4 convolution_bitcast_fusion
  64.5 1.4 convolution_bitcast_fusion.1
  66.0 0.7 reshape.161
  66.7 0.1 copy.76
  66.8 0.6 reshape.146
  67.4 0.1 copy.73
  67.5 0.6 reshape.145
  68.1 6.0 %all-to-all-start = ((f32[16,1,256]{2,1,0:T(1,128)}), f32[16,1,256]{2,1,0:T(1,128)S(1)}, u32[]{:S(2)}, u32[]{:S(2)}) async-start(f32[16,1,256]{2,1,0:T(1,128)} %reshape.161), calls=%async_computation | async-start | bytes 32768 | tf_op jit(solution)/shard_map/all_to_all | solution.py:120
  74.2 1.5 %pad_maximum_fusion = f32[16,2,2,8192]{3,2,0,1:T(2,128)S(1)} fusion(f32[16,1,2,8192]{3,2,0,1:T(2,128)S(1)} %reshape.146, f32[16,1,2,8192]{3,2,0,1:T(2,128)S(1)} %reshape.145), kind=kLoop, calls=%fused_computation.3 | loop fusion | flops 524288 | bytes 4194304 | tf_op jit(solution)/shard_map/while/body/eval_jaxpr/stack | solution.py:98
  75.7 1.2 copy.77
  76.9 2.7 %copy.78 = f32[16,4,8192]{2,1,0:T(4,128)} copy(f32[16,4,8192]{2,0,1:T(8,128)S(1)} %bitcast.93) | data formatting | bytes 4194304 | tf_op jit(solution)/shard_map/all_to_all | solution.py:122
  79.6 6.0 %all-to-all-start.1 = ((f32[16,4,8192]{2,1,0:T(4,128)}), f32[16,4,8192]{2,1,0:T(4,128)}, u32[]{:S(2)}, u32[]{:S(2)}) async-start(f32[16,4,8192]{2,1,0:T(4,128)} %copy.78), calls=%async_computation.1 | async-start | bytes 4194304 | tf_op jit(solution)/shard_map/all_to_all | solution.py:122
  85.6 5.6 %fusion.41 = (bf16[3,512,1024]{2,1,0:T(8,128)(2,1)}, bf16[3,512,1024]{2,1,0:T(8,128)(2,1)S(1)}) fusion(bf16[3,512,2048]{2,1,0:T(8,128)(2,1)} %param.8), kind=kLoop, calls=%fused_computation.68 | loop fusion | bytes 12582912 | tf_op jit(solution)/shard_map/slice | solution.py:46
  91.2 3.0 %copy.108 = bf16[3,512,1024]{1,2,0:T(8,128)(2,1)} copy(bf16[3,512,1024]{2,1,0:T(8,128)(2,1)S(1)} %get-tuple-element.28) | data formatting | bytes 6291456
  94.2 3.2 %copy.105 = bf16[3,512,1024]{1,2,0:T(8,128)(2,1)S(1)} copy(bf16[3,512,1024]{2,1,0:T(8,128)(2,1)} %get-tuple-element.20) | data formatting | bytes 6291456
  97.4 0.1 iota_compare_fusion
  97.5 1.4 fusion.43
  99.0 0.1 reshape.144
  99.0 0.2 fusion.19
  99.3 0.1 reshape.151
  99.3 2.8 %convolution_bitcast_fusion.2 = f32[1,3,64,128]{3,2,1,0:T(8,128)S(1)} fusion(bf16[3,512,8,128]{1,3,2,0:T(8,128)(2,1)} %bitcast.92, f32[3,8,8,512]{3,2,1,0:T(8,128)S(1)} %get-tuple-element.36, f32[3,8,8]{2,1,0:T(8,128)S(1)} %get-tuple-element.35, pred[3,512]{1,0:T(4,128)(4,1)S(1)} %iota_compare_fusion), kind=kOutput, calls=%fused_computation.17 | convolution fusion | flops 25460736 | bytes 3639552 | tf_op jit(solution)/shard_map/ckgt,ctkd->ckgd/dot_general | solution.py:57
  102.2 0.5 broadcast.48
  102.7 0.7 reduce.2
  103.4 0.1 reshape.164
  103.5 0.7 reduce.3
  104.2 0.1 reshape.162
  104.3 0.1 subtract_exponential_fusion.3
  104.5 2.0 %mul.73 = f32[16,4,64,128]{3,2,1,0:T(8,128)} broadcast(f32[16,4,64]{2,1,0:T(4,128)S(1)} %get-tuple-element.19), dimensions={0,1,2} | broadcast | bytes 2113536 | tf_op jit(solution)/shard_map/mul | solution.py:131
  106.5 2.1 %mul.74 = f32[16,4,8192]{2,1,0:T(4,128)S(1)} reshape(f32[16,4,64,128]{3,2,1,0:T(8,128)} %mul.73) | data formatting | bytes 4194304 | tf_op jit(solution)/shard_map/mul | solution.py:131
  108.6 0.1 copy.79
  108.7 0.1 fusion.7
  108.8 0.1 copy.86
  108.9 24.3 %all-to-all-done.1 = f32[16,4,8192]{2,1,0:T(4,128)} async-done(((f32[16,4,8192]{2,1,0:T(4,128)}), f32[16,4,8192]{2,1,0:T(4,128)}, u32[]{:S(2)}, u32[]{:S(2)}) %all-to-all-start.1) | async-done | bytes 2097184 | tf_op jit(solution)/shard_map/all_to_all | solution.py:122
  133.2 2.3 %multiply_reduce_fusion = f32[4,8192]{1,0:T(4,128)S(1)} fusion(f32[16,4,8192]{2,1,0:T(4,128)S(1)} %mul.74, f32[16,4,8192]{2,1,0:T(4,128)} %all-to-all-done.1), kind=kLoop, calls=%fused_computation.4 | loop fusion | flops 1015808 | bytes 4325376 | tf_op jit(solution)/shard_map/reduce_sum | solution.py:131
  135.5 0.3 fusion.6
  135.8 1.6 %multiply_reduce_fusion.1 = (f32[3]{0:T(128)}, bf16[3,8192]{1,0:T(4,128)(2,1)}) fusion(f32[8192]{0:T(1024)S(1)} %copy-done.4, f32[4,8192]{1,0:T(4,128)S(1)} %fusion.6, s32[3]{0:T(128)S(1)} %copy-done.6), kind=kOutput, calls=%fused_computation.42 | convolution fusion | flops 1277961 | bytes 213016 | tf_op jit(solution)/shard_map/cs,sf->cf/dot_general | solution.py:139
  (28 shorter events, 0.2 us)
Async XLA Ops:
  7.2 41.9 %all-gather.3.cloned.1.call-start = ((), (), s32[]{:S(2)}) async-start(), calls=%async_computation.3 | async-start | bytes 1114112 | tf_op jit(solution)/shard_map/all_gather | solution.py:112
  8.7 0.5 copy-start.5
  57.5 10.6 %all-to-all-start.2 = ((f32[16,1,256]{2,1,0:T(1,128)}), f32[16,1,256]{2,1,0:T(1,128)S(1)}, u32[]{:S(2)}, u32[]{:S(2)}) async-start(f32[16,1,256]{2,1,0:T(1,128)} %reshape.163), calls=%async_computation.2 | async-start | bytes 32768 | tf_op jit(solution)/shard_map/all_to_all | solution.py:121
  68.1 8.8 %copy-start = (f32[16,1,256]{2,1,0:T(1,128)}, f32[16,1,256]{2,1,0:T(1,128)S(1)}, u32[]{:S(2)}) copy-start(f32[16,1,256]{2,1,0:T(1,128)S(1)} %all-to-all-done.2) | copy-start | bytes 49156
  68.1 11.5 %all-to-all-start = ((f32[16,1,256]{2,1,0:T(1,128)}), f32[16,1,256]{2,1,0:T(1,128)S(1)}, u32[]{:S(2)}, u32[]{:S(2)}) async-start(f32[16,1,256]{2,1,0:T(1,128)} %reshape.161), calls=%async_computation | async-start | bytes 32768 | tf_op jit(solution)/shard_map/all_to_all | solution.py:120
  79.6 11.6 %copy-start.2 = (f32[16,1,256]{2,1,0:T(1,128)}, f32[16,1,256]{2,1,0:T(1,128)S(1)}, u32[]{:S(2)}) copy-start(f32[16,1,256]{2,1,0:T(1,128)S(1)} %all-to-all-done) | copy-start | bytes 49156
  79.6 53.5 %all-to-all-start.1 = ((f32[16,4,8192]{2,1,0:T(4,128)}), f32[16,4,8192]{2,1,0:T(4,128)}, u32[]{:S(2)}, u32[]{:S(2)}) async-start(f32[16,4,8192]{2,1,0:T(4,128)} %copy.78), calls=%async_computation.1 | async-start | bytes 4194304 | tf_op jit(solution)/shard_map/all_to_all | solution.py:122
  94.2 3.2 %copy-start.7 = (s32[3]{0:T(128)S(1)}, s32[3]{0:T(128)}, u32[]{:S(2)}) copy-start(s32[3]{0:T(128)} %param.9) | copy-start | bytes 40
  99.0 3.8 %copy-start.1 = (f32[16,1,256]{2,1,0:T(1,128)S(1)}, f32[16,1,256]{2,1,0:T(1,128)}, u32[]{:S(2)}) copy-start(f32[16,1,256]{2,1,0:T(1,128)} %copy-done) | copy-start | bytes 49156
  99.0 4.5 %copy-start.3 = (f32[16,1,256]{2,1,0:T(1,128)S(1)}, f32[16,1,256]{2,1,0:T(1,128)}, u32[]{:S(2)}) copy-start(f32[16,1,256]{2,1,0:T(1,128)} %copy-done.2) | copy-start | bytes 49156
  99.0 5.4 %copy-start.6 = (s32[3]{0:T(128)S(1)}, s32[3]{0:T(128)}, u32[]{:S(2)}) copy-start(s32[3]{0:T(128)} %copy-done.5) | copy-start | bytes 40
  108.5 27.2 %copy-start.4 = (f32[8192]{0:T(1024)S(1)}, f32[8192]{0:T(1024)}, u32[]{:S(2)}) copy-start(f32[8192]{0:T(1024)} %param.11) | copy-start | bytes 98308
Sparse Core Ops, SparseCore 0:
  11.0 37.9 all-gather.2
where the time goes:
time: 145 us; the launch traced here: 144 us
  waiting for transfers between devices  59.1 us (41%)
  local copies, waits for them, and re-layouts  33 us (23%)
  starting transfers between devices  17.5 us (12%)
  between operations  14.4 us (10%)
  matrix products  12.7 us (9%)
  other arithmetic  7.54 us (5%)
    all_gather x1, waiting for transfers between devices, body(): query_rows = (lax.all_gather(row_block, 'seq', axis=0, tiled=True),)[0]  34.8 us
    all_to_all x1, waiting for transfers between devices, body(): lax.all_to_all(computed[2], 'seq', split_axis=0, concat_axis=0, tiled=True)  24.3 us
    unnamed x27, local copies, waits for them, and re-layouts  11.6 us
    all_to_all x1, starting transfers between devices, body(): lax.all_to_all(computed[0], 'seq', split_axis=0, concat_axis=0, tiled=True)  6.03 us
    all_to_all x1, starting transfers between devices, body(): lax.all_to_all(computed[2], 'seq', split_axis=0, concat_axis=0, tiled=True)  6.02 us
    slice x1, local copies, waits for them, and re-layouts, body(): suffix_cache[:, :, :kv_width].reshape(cand_rows, suffix_len, kv_heads, HD)  5.57 us
    all_to_all x1, starting transfers between devices, body(): lax.all_to_all(computed[1], 'seq', split_axis=0, concat_axis=0, tiled=True)  5.37 us
    mul x2, local copies, waits for them, and re-layouts, body(): factor[..., None] * back_mix  4.05 us
  transfers between devices with their start and end apart: 4, of which 2 were waited for; matrix products, arithmetic and copies ran while one was open for 26% of the time, Pallas kernels for 0%

commit v1 on v0

v1 whole, which is shorter than its diff:
```python
import math

import jax
import jax.numpy as jnp
from jax import lax
from jax.experimental import pallas as pl
from jax.experimental.pallas import tpu as pltpu
from jax.sharding import PartitionSpec as P

HD = 128
BLOCK = 128
SLAB = 4
F32 = jnp.float32
BF16 = jnp.bfloat16
floor_logit = -1e30


def vmem_spec():
    return pl.BlockSpec(memory_space=pltpu.VMEM)


def split3(x):
    high = x.astype(BF16).astype(F32)
    rest = x - high
    middle = rest.astype(BF16).astype(F32)
    low = (rest - middle).astype(BF16).astype(F32)
    return [high, middle, low]


def pack_stats(pairs):
    rows = []
    for maximum, total in pairs:
        rows += split3(maximum) + split3(total) + [jnp.zeros((2, HD), F32)]
    return jnp.concatenate(rows, axis=0)


def unpack_stats(stats, k):
    at = 8 * k
    maximum = stats[at : at + 1] + stats[at + 1 : at + 2] + stats[at + 2 : at + 3]
    total = stats[at + 3 : at + 4] + stats[at + 4 : at + 5] + stats[at + 5 : at + 6]
    return maximum, total


def to_lanes(column):
    rows = column.shape[0]
    same = lax.broadcasted_iota(jnp.int32, (rows, HD), 0) == lax.broadcasted_iota(
        jnp.int32, (rows, HD), 1
    )
    return jnp.sum(jnp.where(same, jnp.broadcast_to(column, (rows, HD)), 0.0), axis=0, keepdims=True)


def to_rows(lanes, rows, offset):
    same = lax.broadcasted_iota(jnp.int32, (rows, HD), 0) + offset == lax.broadcasted_iota(
        jnp.int32, (rows, HD), 1
    )
    return jnp.sum(jnp.where(same, jnp.broadcast_to(lanes, (rows, HD)), 0.0), axis=1, keepdims=True)


def prepare(me, queries, prompt_of, prompt_cache, kvq, group):
    cands, width = queries.shape
    heads = width // HD
    prompts, span, kv_width2 = prompt_cache.shape
    kv_width = kv_width2 // 2
    hq = kvq * group
    part_rows = kvq * cands * group + 8
    kvw = kvq * HD

    def kernel(me_ref, q_ref, ids_ref, cache_ref, all_ref, *rest):
        q_out = rest[:SLAB]
        kv_out = rest[SLAB : 2 * SLAB]
        scratch, sem = rest[2 * SLAB :]
        mine = me_ref[0]
        copies = []
        for j in range(SLAB):
            column = pl.multiple_of((mine ^ j) * kvw, kvw)
            for side in range(2):
                copy = pltpu.make_async_copy(
                    cache_ref.at[:, :, pl.ds(side * kv_width + column, kvw)],
                    kv_out[j].at[side],
                    sem.at[j, side],
                )
                copy.start()
                copies.append(copy)
        for h in range(heads):
            scratch[pl.ds(h, cands, stride=heads), :] = q_ref[:, h * HD : (h + 1) * HD].astype(F32)
        all_ref[...] = scratch[...].astype(BF16)
        id_rows = [jnp.full((1, HD), ids_ref[r, 0].astype(F32)) for r in range(cands)]
        id_rows = id_rows + [jnp.zeros((8 - cands, HD), F32)]
        for j in range(SLAB):
            first = (mine ^ j) * hq
            pieces = []
            for k in range(kvq):
                for r in range(cands):
                    at = pl.multiple_of(r * heads + first + k * group, 8)
                    pieces.append(scratch[pl.ds(at, group), :])
            q_out[j][...] = jnp.concatenate(pieces + id_rows, axis=0).astype(BF16)
        for copy in copies:
            copy.wait()

    smem = pl.BlockSpec(memory_space=pltpu.SMEM)
    hbm = pl.BlockSpec(memory_space=pl.ANY)
    out = pl.pallas_call(
        kernel,
        out_shape=[jax.ShapeDtypeStruct((cands * heads, HD), BF16)]
        + [jax.ShapeDtypeStruct((part_rows, HD), BF16)] * SLAB
        + [jax.ShapeDtypeStruct((2, prompts, span, kvw), BF16)] * SLAB,
        in_specs=[smem, vmem_spec(), smem, hbm],
        out_specs=[vmem_spec()] * (1 + SLAB) + [hbm] * SLAB,
        scratch_shapes=[
            pltpu.VMEM((cands * heads, HD), F32),
            pltpu.SemaphoreType.DMA((SLAB, 2)),
        ],
        name="prepare",
    )(me, queries, prompt_of, prompt_cache)
    return out[0], out[1 : 1 + SLAB], out[1 + SLAB :]


def suffix_attend(blocks, rows_q, suffix_cache, kv_heads):
    cands, length, kv_width2 = suffix_cache.shape
    kv_width = kv_width2 // 2
    heads = rows_q.shape[0] // cands
    group = heads // kv_heads

    def kernel(blocks_ref, q_ref, key_ref, value_ref, max_ref, sum_ref, mix_ref):
        q = q_ref[...]
        wide = jnp.concatenate([q] * kv_heads, axis=1)
        diagonal = (
            lax.broadcasted_iota(jnp.int32, (heads, kv_width), 0) // group
            == lax.broadcasted_iota(jnp.int32, (heads, kv_width), 1) // HD
        )
        wide = jnp.where(diagonal, wide, jnp.zeros_like(wide))
        logits = lax.dot_general(
            wide, key_ref[0], (((1,), (1,)), ((), ())), preferred_element_type=F32
        ) * HD ** (-0.5)
        live = (
            lax.broadcasted_iota(jnp.int32, (heads, length), 1)
            < BLOCK * blocks_ref[pl.program_id(0)]
        )
        logits = jnp.where(live, logits, floor_logit)
        maxima = jnp.max(logits, axis=1, keepdims=True)
        exponent = jnp.where(live, jnp.exp(logits - maxima), 0.0)
        totals = jnp.sum(exponent, axis=1, keepdims=True)
        mixed = jnp.dot(exponent.astype(BF16), value_ref[0], preferred_element_type=F32)
        max_ref[...] = jnp.broadcast_to(maxima, (heads, HD))
        sum_ref[...] = jnp.broadcast_to(totals, (heads, HD))
        for k in range(kv_heads):
            mix_ref[k * group : (k + 1) * group, :] = mixed[
                k * group : (k + 1) * group, k * HD : (k + 1) * HD
            ]

    shape = jax.ShapeDtypeStruct((cands * heads, HD), F32)
    row_spec = pl.BlockSpec((heads, HD), lambda c, b: (c, 0))
    return pl.pallas_call(
        kernel,
        out_shape=[shape] * 3,
        grid_spec=pltpu.PrefetchScalarGridSpec(
            num_scalar_prefetch=1,
            grid=(cands,),
            in_specs=[
                row_spec,
                pl.BlockSpec((1, length, kv_width), lambda c, b: (c, 0, 0)),
                pl.BlockSpec((1, length, kv_width), lambda c, b: (c, 0, 1)),
            ],
            out_specs=[row_spec] * 3,
        ),
        cost_estimate=pl.CostEstimate(
            flops=4 * cands * heads * length * kv_width,
            transcendentals=cands * heads * length,
            bytes_accessed=2 * suffix_cache.size,
        ),
        name="suffix",
    )(blocks, rows_q, suffix_cache, suffix_cache)


def prompt_attend(query_blocks, caches, cands, kvq, group):
    stacked = not isinstance(query_blocks, list)
    outer = query_blocks.shape[0] if stacked else len(query_blocks)
    chunk = math.gcd(outer, 4)
    part = cands * group
    part_rows = kvq * part + 8
    block_rows = SLAB * part
    out_rows = kvq * block_rows + 8 * kvq
    prompts, span = caches[0].shape[1:3]
    width = SLAB * span

    def kernel(*refs):
        if stacked:
            q_refs = [refs[0].at[i] for i in range(chunk)]
            cache_refs = refs[1 : 1 + SLAB]
            out_refs = [refs[1 + SLAB].at[i] for i in range(chunk)]
        else:
            q_refs = refs[:chunk]
            cache_refs = refs[chunk : chunk + SLAB]
            out_refs = refs[chunk + SLAB :]
        rows = [q_ref[...].astype(F32) for q_ref in q_refs]
        ids = []
        for i in range(chunk):
            for j in range(SLAB):
                for r in range(cands):
                    at = j * part_rows + kvq * part + r
                    ids.append(jnp.broadcast_to(rows[i][at : at + 1], (group, HD)))
        ids = jnp.concatenate(ids, axis=0)
        ids = jnp.concatenate([ids] * (width // HD), axis=1)
        picked = [ids == float(p) for p in range(prompts)]
        stats = [[] for i in range(chunk)]
        for k in range(kvq):
            q = jnp.concatenate(
                [
                    rows[i][j * part_rows + k * part : j * part_rows + (k + 1) * part]
                    for i in range(chunk)
                    for j in range(SLAB)
                ],
                axis=0,
            ).astype(BF16)
            logits = None
            for p in range(prompts):
                keys = jnp.concatenate(
                    [ref[0, p, :, k * HD : (k + 1) * HD] for ref in cache_refs], axis=0
                )
                one = lax.dot_general(
                    q, keys, (((1,), (1,)), ((), ())), preferred_element_type=F32
                )
                logits = one if logits is None else jnp.where(picked[p], one, logits)
            logits = logits * HD ** (-0.5)
            maxima = jnp.max(logits, axis=1, keepdims=True)
            exponent = jnp.exp(logits - maxima)
            totals = jnp.sum(exponent, axis=1, keepdims=True)
            mixed = None
            for p in range(prompts):
                values = jnp.concatenate(
                    [ref[1, p, :, k * HD : (k + 1) * HD] for ref in cache_refs], axis=0
                )
                weights = jnp.where(picked[p], exponent, 0.0).astype(BF16)
                one = jnp.dot(weights, values, preferred_element_type=F32)
                mixed = one if mixed is None else mixed + one
            for i in range(chunk):
                cut = slice(i * block_rows, (i + 1) * block_rows)
                out_refs[i][k * block_rows : (k + 1) * block_rows, :] = mixed[cut].astype(BF16)
                stats[i].append((to_lanes(maxima[cut]), to_lanes(totals[cut])))
        for i in range(chunk):
            out_refs[i][kvq * block_rows :, :] = pack_stats(stats[i]).astype(BF16)

    if stacked:
        whole = [
            pl.BlockSpec(c.shape, lambda s: (0, 0, 0, 0)) for c in caches
        ]
        return pl.pallas_call(
            kernel,
            out_shape=jax.ShapeDtypeStruct((outer, out_rows, HD), BF16),
            grid=(outer // chunk,),
            in_specs=[pl.BlockSpec((chunk, SLAB * part_rows, HD), lambda s: (s, 0, 0))] + whole,
            out_specs=pl.BlockSpec((chunk, out_rows, HD), lambda s: (s, 0, 0)),
            name="prompt",
        )(query_blocks, *caches)
    return pl.pallas_call(
        kernel,
        out_shape=[jax.ShapeDtypeStruct((out_rows, HD), BF16)] * outer,
        in_specs=[vmem_spec()] * (outer + SLAB),
        out_specs=[vmem_spec()] * outer,
        name="prompt",
    )(*query_blocks, *caches)


def merge(blocks, cands, kvq, group):
    stacked = not isinstance(blocks, list)
    outer = blocks.shape[0] if stacked else len(blocks)
    part = cands * group
    block_rows = SLAB * part
    out_rows = kvq * part + 8 * kvq

    def kernel(*refs):
        if stacked:
            in_refs = [refs[0].at[i] for i in range(outer)]
            out_refs = refs[1:]
        else:
            in_refs = refs[:outer]
            out_refs = refs[outer:]
        stats = [ref[kvq * block_rows :, :].astype(F32) for ref in in_refs]
        merged = []
        for k in range(kvq):
            pairs = [unpack_stats(one, k) for one in stats]
            joined = pairs[0][0]
            for maximum, total in pairs[1:]:
                joined = jnp.maximum(joined, maximum)
            total_all = jnp.zeros((1, HD), F32)
            mixed = jnp.zeros((block_rows, HD), F32)
            for (maximum, total), ref in zip(pairs, in_refs):
                factor = jnp.exp(maximum - joined)
                total_all = total_all + factor * total
                mixed = mixed + to_rows(factor, block_rows, 0) * ref[
                    k * block_rows : (k + 1) * block_rows, :
                ].astype(F32)
            merged.append((joined, total_all))
            for j in range(SLAB):
                out_refs[j][k * part : (k + 1) * part, :] = mixed[
                    j * part : (j + 1) * part
                ].astype(BF16)
        packed = pack_stats(merged).astype(BF16)
        for j in range(SLAB):
            out_refs[j][kvq * part :, :] = packed

    args = [blocks] if stacked else blocks
    return pl.pallas_call(
        kernel,
        out_shape=[jax.ShapeDtypeStruct((out_rows, HD), BF16)] * SLAB,
        in_specs=[vmem_spec()] * len(args),
        out_specs=[vmem_spec()] * SLAB,
        name="merge",
    )(*args)


def finish(me, pieces, suffix_state, reward, cands, kvq, group):
    part = cands * group
    hq = kvq * group
    heads = SLAB * hq

    def kernel(me_ref, *refs):
        piece_refs = refs[:SLAB]
        max_ref, sum_ref, mix_ref, reward_ref, out_ref, score_ref, scratch = refs[SLAB:]
        mine = me_ref[0]
        scores = [jnp.zeros((group, HD), F32) for r in range(cands)]
        for j in range(SLAB):
            first = (mine ^ j) * hq
            stats = piece_refs[j][kvq * part :, :].astype(F32)
            mix = piece_refs[j][: kvq * part, :].astype(F32)
            for k in range(kvq):
                maximum, total = unpack_stats(stats, k)
                maximum = to_rows(maximum, part, j * part)
                total = to_rows(total, part, j * part)
                weight = reward_ref[pl.ds(pl.multiple_of(first + k * group, 8), group), :]
                for r in range(cands):
                    at = pl.ds(pl.multiple_of(r * heads + first + k * group, 8), group)
                    cut = slice(r * group, (r + 1) * group)
                    home_max = max_ref[at, :]
                    here_max = jnp.broadcast_to(maximum[cut], (group, HD))
                    joined = jnp.maximum(home_max, here_max)
                    home = jnp.exp(home_max - joined)
                    here = jnp.exp(here_max - joined)
                    total_all = home * sum_ref[at, :] + here * total[cut]
                    mixed = home * mix_ref[at, :] + here * mix[k * part :][cut]
                    attended = (mixed / total_all).astype(BF16).astype(F32)
                    scratch[at, :] = attended
                    scores[r] = scores[r] + attended * weight
        for h in range(heads):
            out_ref[:, h * HD : (h + 1) * HD] = scratch[pl.ds(h, cands, stride=heads), :].astype(
                BF16
            )
        for r in range(cands):
            score_ref[r] = jnp.sum(scores[r])

    smem = pl.BlockSpec(memory_space=pltpu.SMEM)
    return pl.pallas_call(
        kernel,
        out_shape=[
            jax.ShapeDtypeStruct((cands, heads * HD), BF16),
            jax.ShapeDtypeStruct((cands,), F32),
        ],
        in_specs=[smem] + [vmem_spec()] * (SLAB + 4),
        out_specs=[vmem_spec(), smem],
        scratch_shapes=[pltpu.VMEM((cands * heads, HD), F32)],
        name="finish",
    )(me, *pieces, *suffix_state, reward)


def body(queries, prompt_of, suffix_cache, suffix_blocks, prompt_cache, reward_weight):
    cands = queries.shape[0]
    heads = queries.shape[1] // HD
    kv_heads = prompt_cache.shape[2] // (2 * HD)
    group = heads // kv_heads
    kvq = kv_heads // SLAB
    devices = lax.axis_size("seq")
    outer = devices // SLAB
    me = jnp.reshape(lax.axis_index("seq") % SLAB, (1,)).astype(jnp.int32)

    def hop(x, step):
        return lax.ppermute(x, "seq", [(i, i ^ step) for i in range(devices)])

    direct = outer <= 4 and outer & (outer - 1) == 0
    columns = [[SLAB * z + i for z in range(outer)] for i in range(SLAB)]

    rows_q, q_parts, kv_parts = prepare(me, queries, prompt_of, prompt_cache, kvq, group)
    q_parts = [q_parts[0]] + [hop(q_parts[j], j) for j in range(1, SLAB)]
    kv_parts = [kv_parts[0]] + [hop(kv_parts[j], j) for j in range(1, SLAB)]
    q_slab = jnp.concatenate(q_parts, axis=0)
    rows_q, q_slab = lax.optimization_barrier((rows_q, q_slab))
    suffix_state = suffix_attend(suffix_blocks, rows_q, suffix_cache, kv_heads)
    if direct:
        q_all = [q_slab] + [hop(q_slab, SLAB * i) for i in range(1, outer)]
    else:
        q_all = lax.all_gather(q_slab, "seq", axis_index_groups=columns)
    partial = prompt_attend(q_all, kv_parts, cands, kvq, group)
    if direct:
        partial = [partial[0]] + [hop(partial[i], SLAB * i) for i in range(1, outer)]
    else:
        partial = lax.all_to_all(
            partial, "seq", split_axis=0, concat_axis=0, axis_index_groups=columns, tiled=True
        )
    pieces = merge(partial, cands, kvq, group)
    pieces = [pieces[0]] + [hop(pieces[j], j) for j in range(1, SLAB)]
    reward = reward_weight.reshape(heads, HD)
    return tuple(finish(me, pieces, suffix_state, reward, cands, kvq, group))


def solution(mesh):
    placed = (
        P(("groups", "seq"), None),
        P(("groups", "seq"), None),
        P(("groups", "seq"), None, None),
        P(("groups", "seq")),
        P("groups", "seq", None),
        P(),
    )
    return jax.shard_map(
        body,
        mesh=mesh,
        in_specs=placed,
        out_specs=(P(("groups", "seq"), None), P(("groups", "seq"))),
        check_vma=False,
    )
```

time: 145 us -> 89.9 us (0.62)
  the two profiles are of different devices: /device:TPU:13 before, /device:TPU:0 now
where the time goes in v1:
time: 89.9 us; the launch traced here: 89.6 us
  Pallas kernels  47.5 us (53%)
  starting transfers between devices  21.1 us (23%)
  waiting for transfers between devices  16 us (18%)
  local copies, waits for them, and re-layouts  3.38 us (4%)
    pallas_call x1, Pallas kernels, prepare(): pl.pallas_call(kernel, out_shape=[jax.ShapeDtypeStruct((cands * heads, HD...  34.4 us
    ppermute x15, starting transfers between devices, hop(): return lax.ppermute(x, 'seq', [(i, i ^ step) for i in range(devices)])  21.1 us
    ppermute x15, waiting for transfers between devices, hop(): return lax.ppermute(x, 'seq', [(i, i ^ step) for i in range(devices)])  16 us
    pallas_call x1, Pallas kernels, suffix_attend(): pl.pallas_call(kernel, out_shape=[shape] * 3, grid_spec=pltpu.PrefetchSca...  6 us
    pallas_call x1, Pallas kernels, prompt_attend(): pl.pallas_call(kernel, out_shape=[jax.ShapeDtypeStruct((out_rows, HD), BF...  3.48 us
    unnamed x27, local copies, waits for them, and re-layouts  3.38 us
    pallas_call x1, Pallas kernels, finish(): pl.pallas_call(kernel, out_shape=[jax.ShapeDtypeStruct((cands, heads * HD...  1.93 us
  transfers between devices with their start and end apart: 15, of which 5 were waited for; matrix products, arithmetic and copies ran while one was open for 1% of the time, Pallas kernels for 7%

profile of v1, /device:TPU:0, one launch (start us, length us, event | category | flops | bytes accessed | tf_op | source)
XLA Modules:
  0.0 89.6 jit_solution(16534931779387577592)
XLA Ops:
  0.6 1.3 %copy.8.ids_ref = s32[3,1]{1,0:T(4,128)} copy(s32[3,1]{0,1:T(1,128)} %param.7) | data formatting | bytes 24 | tf_op args[1]
  1.9 34.4 %prepare.1 = (bf16[192,128]{1,0:T(8,128)(2,1)}, bf16[56,128]{1,0:T(8,128)(2,1)}, bf16[56,128]{1,0:T(8,128)(2,1)}, bf16[56,128]{1,0:T(8,128)(2,1)}, bf16[56,128]{...) custom-call(s32[1]{0:T(128)} %bitcast.me_ref, ...), custom_call_target="tpu_custom_call" | custom-call | tf_op jit(solution)/shard_map/prepare/pallas_call | solution.py:102
  36.4 0.6 collective-permute-start.6
  36.9 2.6 %collective-permute-start.7 = (bf16[2,2,128,256]{3,2,1,0:T(8,128)(2,1)}, bf16[2,2,128,256]{3,2,1,0:T(8,128)(2,1)S(1)}, u32[]{:S(2)}, u32[]{:S(2)}) collective-permute-start(bf16[2,2,128,256]{3,2,1,0:T(8,128)(2,1)} %get-tuple-element.32), channel_id=1, source_target_pairs={{0,2},{1,3},{2,0},{3,1},{4,6},{5,7},{6,4},{7,5},{8,10},{9,11},{10,... | collective-permute-start | bytes 786440 | tf_op jit(solution)/shard_map/ppermute | solution.py:376
  39.5 0.0 collective-permute-start.8
  39.6 0.2 collective-permute-start
  39.7 1.9 %collective-permute-start.1 = (bf16[56,128]{1,0:T(8,128)(2,1)}, bf16[56,128]{1,0:T(8,128)(2,1)S(1)}, u32[]{:S(2)}, u32[]{:S(2)}) collective-permute-start(bf16[56,128]{1,0:T(8,128)(2,1)} %get-tuple-element.27), channel_id=1, source_target_pairs={{0,2},{1,3},{2,0},{3,1},{4,6},{5,7},{6,4},{7,5},{8,10},{9,11},{10,... | collective-permute-start | bytes 43016 | tf_op jit(solution)/shard_map/ppermute | solution.py:376
  41.7 0.0 collective-permute-done
  41.7 1.0 %collective-permute-start.2 = (bf16[56,128]{1,0:T(8,128)(2,1)}, bf16[56,128]{1,0:T(8,128)(2,1)S(1)}, u32[]{:S(2)}, u32[]{:S(2)}) collective-permute-start(bf16[56,128]{1,0:T(8,128)(2,1)} %get-tuple-element.28), channel_id=1, source_target_pairs={{0,3},{1,2},{2,1},{3,0},{4,7},{5,6},{6,5},{7,4},{8,11},{9,10},{10,... | collective-permute-start | bytes 43016 | tf_op jit(solution)/shard_map/ppermute | solution.py:376
  42.7 10.0 %collective-permute-done.1 = bf16[56,128]{1,0:T(8,128)(2,1)S(1)} collective-permute-done((bf16[56,128]{1,0:T(8,128)(2,1)}, bf16[56,128]{1,0:T(8,128)(2,1)S(1)}, u32[]{:S(2)}, u32[]{:S(2)}) %collective-permute-start.1) | collective-permute-done | bytes 14368 | tf_op jit(solution)/shard_map/ppermute | solution.py:376
  52.7 0.0 collective-permute-done.2
  52.7 0.7 pad_maximum_fusion.refs_0_
  53.4 0.0 copy-start.3
  53.4 1.8 %collective-permute-start.3 = (bf16[224,128]{1,0:T(8,128)(2,1)S(1)}, bf16[224,128]{1,0:T(8,128)(2,1)S(1)}, u32[]{:S(2)}, u32[]{:S(2)}) collective-permute-start(bf16[224,128]{1,0:T(8,128)(2,1)S(1)} %pad_maximum_fusion.refs_0_), channel_id=1, source_target_pairs={{0,4},{1,5},{2,6},{3,7},{4,0},{5,1},{6,2},{7,3},{8,12},{9,13},{10,... | collective-permute-start | bytes 172040 | tf_op jit(solution)/shard_map/ppermute | solution.py:376
  55.2 2.6 %collective-permute-start.4 = (bf16[224,128]{1,0:T(8,128)(2,1)S(1)}, bf16[224,128]{1,0:T(8,128)(2,1)S(1)}, u32[]{:S(2)}, u32[]{:S(2)}) collective-permute-start(bf16[224,128]{1,0:T(8,128)(2,1)S(1)} %pad_maximum_fusion.refs_0_), channel_id=1, source_target_pairs={{0,8},{1,9},{2,10},{3,11},{4,12},{5,13},{6,14},{7,15},{8,0},{9,1},... | collective-permute-start | bytes 172040 | tf_op jit(solution)/shard_map/ppermute | solution.py:376
  57.8 0.0 collective-permute-done.3.refs_1_
  57.8 0.0 copy-start.4
  57.8 4.2 %collective-permute-start.5 = (bf16[224,128]{1,0:T(8,128)(2,1)S(1)}, bf16[224,128]{1,0:T(8,128)(2,1)S(1)}, u32[]{:S(2)}, u32[]{:S(2)}) collective-permute-start(bf16[224,128]{1,0:T(8,128)(2,1)S(1)} %pad_maximum_fusion.refs_0_), channel_id=1, source_target_pairs={{0,12},{1,13},{2,14},{3,15},{4,8},{5,9},{6,10},{7,11},{8,4},{9,5},... | collective-permute-start | bytes 172040 | tf_op jit(solution)/shard_map/ppermute | solution.py:376
  62.0 0.0 collective-permute-done.4.refs_2_
  62.1 0.0 copy-start.5
  62.1 2.1 %collective-permute-done.5.refs_3_ = bf16[224,128]{1,0:T(8,128)(2,1)S(1)} collective-permute-done((bf16[224,128]{1,0:T(8,128)(2,1)S(1)}, bf16[224,128]{1,0:T(8,128)(2,1)S(1)}, u32[]{:S(2)}, u32[]{:S(2)}) %collective-permute-start.5) | collective-permute-done | bytes 57376 | tf_op jit(solution)/shard_map/ppermute | solution.py:376
  64.2 0.0 copy-start.6
  64.2 0.0 collective-permute-done.6.refs_5_
  64.2 0.0 copy-start
  64.2 0.0 collective-permute-done.7.refs_6_
  64.2 0.0 copy-start.1
  64.2 0.0 collective-permute-done.8.refs_7_
  64.2 0.0 copy-start.2
  64.2 0.0 copy-done.3
  64.3 0.0 copy-done.4
  64.3 0.0 copy-done.5
  64.3 0.5 copy-done.6
  64.8 0.1 copy-done
  64.9 0.1 copy-done.1
  65.0 0.1 copy-done.2
  65.1 3.5 %prompt.1 = (bf16[208,128]{1,0:T(8,128)(2,1)}, bf16[208,128]{1,0:T(8,128)(2,1)}, bf16[208,128]{1,0:T(8,128)(2,1)}, bf16[208,128]{1,0:T(8,128)(2,1)}) custom-call(bf16[224,128]{1,0:T(8,128)(2,1)} %copy-done.3, bf16[224,128]{1,0:T(8,128)(2,1)} %copy-done.4, bf16[224,128]{1,0:T(8,128)(2,1)} %copy-done.5, bf16[224,128]{1,0:T(8,128)(2,1)} %copy-done.6, ...), custom_call_target="tpu_custom_call" | custom-call | tf_op jit(solution)/shard_map/prompt/pallas_call | solution.py:255
  68.6 0.9 %collective-permute-start.10 = (bf16[208,128]{1,0:T(8,128)(2,1)}, bf16[208,128]{1,0:T(8,128)(2,1)S(1)}, u32[]{:S(2)}, u32[]{:S(2)}) collective-permute-start(bf16[208,128]{1,0:T(8,128)(2,1)} %get-tuple-element.36), channel_id=1, source_target_pairs={{0,8},{1,9},{2,10},{3,11},{4,12},{5,13},{6,14},{7,15},{8,0},{9,1},... | collective-permute-start | bytes 159752 | tf_op jit(solution)/shard_map/ppermute | solution.py:376
  69.5 3.0 %collective-permute-start.11 = (bf16[208,128]{1,0:T(8,128)(2,1)}, bf16[208,128]{1,0:T(8,128)(2,1)S(1)}, u32[]{:S(2)}, u32[]{:S(2)}) collective-permute-start(bf16[208,128]{1,0:T(8,128)(2,1)} %get-tuple-element.37), channel_id=1, source_target_pairs={{0,12},{1,13},{2,14},{3,15},{4,8},{5,9},{6,10},{7,11},{8,4},{9,5},... | collective-permute-start | bytes 159752 | tf_op jit(solution)/shard_map/ppermute | solution.py:376
  72.5 0.5 collective-permute-start.9
  73.0 0.9 collective-permute-done.10.refs_2_
  73.8 0.0 copy-start.7
  73.8 1.8 %collective-permute-done.11.refs_3_ = bf16[208,128]{1,0:T(8,128)(2,1)S(1)} collective-permute-done((bf16[208,128]{1,0:T(8,128)(2,1)}, bf16[208,128]{1,0:T(8,128)(2,1)S(1)}, u32[]{:S(2)}, u32[]{:S(2)}) %collective-permute-start.11) | collective-permute-done | bytes 53280 | tf_op jit(solution)/shard_map/ppermute | solution.py:376
  75.6 0.0 copy-start.8
  75.6 1.2 %collective-permute-done.9.refs_1_ = bf16[208,128]{1,0:T(8,128)(2,1)S(1)} collective-permute-done((bf16[208,128]{1,0:T(8,128)(2,1)}, bf16[208,128]{1,0:T(8,128)(2,1)S(1)}, u32[]{:S(2)}, u32[]{:S(2)}) %collective-permute-start.9) | collective-permute-done | bytes 53280 | tf_op jit(solution)/shard_map/ppermute | solution.py:376
  76.8 0.0 copy-start.9
  76.8 0.0 copy-done.7
  76.8 0.0 copy-done.8
  76.8 0.6 copy-done.9
  77.4 1.7 %merge.1 = (bf16[64,128]{1,0:T(8,128)(2,1)}, bf16[64,128]{1,0:T(8,128)(2,1)}, bf16[64,128]{1,0:T(8,128)(2,1)}, bf16[64,128]{1,0:T(8,128)(2,1)}) custom-call(bf16[208,128]{1,0:T(8,128)(2,1)} %get-tuple-element.34.refs_0_, bf16[208,128]{1,0:T(8,128)(2,1)} %copy-done.9, bf16[208,128]{1,0:T(8,128)(2,1)} %copy-done.7, bf16[208,128]{1,0:T(8,128)(2,1)} %copy-done.8), custom_call_target="tpu_custom_call" | custom-call | tf_op jit(solution)/shard_map/merge/pallas_call | solution.py:303
  79.1 0.0 collective-permute-start.12
  79.1 1.6 %collective-permute-start.13 = (bf16[64,128]{1,0:T(8,128)(2,1)}, bf16[64,128]{1,0:T(8,128)(2,1)S(1)}, u32[]{:S(2)}, u32[]{:S(2)}) collective-permute-start(bf16[64,128]{1,0:T(8,128)(2,1)} %get-tuple-element.40), channel_id=1, source_target_pairs={{0,2},{1,3},{2,0},{3,1},{4,6},{5,7},{6,4},{7,5},{8,10},{9,11},{10,... | collective-permute-start | bytes 49160 | tf_op jit(solution)/shard_map/ppermute | solution.py:376
  80.7 0.3 collective-permute-start.14
  81.0 6.0 %suffix.1 = (f32[192,128]{1,0:T(8,128)}, f32[192,128]{1,0:T(8,128)}, f32[192,128]{1,0:T(8,128)}) custom-call(s32[3]{0:T(128)} %blocks_ref.1, bf16[192,128]{1,0:T(8,128)(2,1)} %get-tuple-element.42.q_ref, bf16[3,512,2048]{2,1,0:T(8,128)(2,1)} %value_ref.1, bf16[3,512,2048]{2,1,0:T(8,128)(2,1)} %value_ref.1), custom_call_target="tpu_custom_call" | custom-call | flops 402653184 | bytes 6291456 | tf_op jit(solution)/shard_map/suffix/pallas_call | solution.py:153
  87.0 0.0 collective-permute-done.12.refs_1_
  87.0 0.0 copy-start.10
  87.0 0.0 collective-permute-done.13.refs_2_
  87.0 0.0 copy-start.11
  87.0 0.0 collective-permute-done.14.refs_3_
  87.0 0.0 copy-start.12
  87.0 0.6 copy-done.10
  87.6 0.0 copy-done.11
  87.6 0.0 copy-done.12
  87.6 1.9 %finish.1 = (bf16[3,8192]{1,0:T(4,128)(2,1)}, f32[3]{0:T(128)}) custom-call(s32[1]{0:T(128)} %bitcast.me_ref, bf16[64,128]{1,0:T(8,128)(2,1)} %get-tuple-element.38.refs_0_, bf16[64,128]{1,0:T(8,128)(2,1)} %copy-done.10, bf16[64,128]{1,0:T(8,128)(2,1)} %copy-done.11, bf16[64,128]{1,0:T(8,128)(2,1)} %copy-done.12, f32[192,128]{1,0:T(8,128)} %get-tuple-element.43.refs_4_, ...), custom_call_target="tpu_custom_call" | custom-call | tf_op jit(solution)/shard_map/finish/pallas_call | solution.py:352
Async XLA Ops:
  36.4 27.8 %collective-permute-start.6 = (bf16[2,2,128,256]{3,2,1,0:T(8,128)(2,1)}, bf16[2,2,128,256]{3,2,1,0:T(8,128)(2,1)S(1)}, u32[]{:S(2)}, u32[]{:S(2)}) collective-permute-start(bf16[2,2,128,256]{3,2,1,0:T(8,128)(2,1)} %get-tuple-element.31), channel_id=1, source_target_pairs={{0,1},{1,0},{2,3},{3,2},{4,5},{5,4},{6,7},{7,6},{8,9},{9,8},{10,11... | collective-permute-start | bytes 786440 | tf_op jit(solution)/shard_map/ppermute | solution.py:376
  36.9 27.3 %collective-permute-start.7 = (bf16[2,2,128,256]{3,2,1,0:T(8,128)(2,1)}, bf16[2,2,128,256]{3,2,1,0:T(8,128)(2,1)S(1)}, u32[]{:S(2)}, u32[]{:S(2)}) collective-permute-start(bf16[2,2,128,256]{3,2,1,0:T(8,128)(2,1)} %get-tuple-element.32), channel_id=1, source_target_pairs={{0,2},{1,3},{2,0},{3,1},{4,6},{5,7},{6,4},{7,5},{8,10},{9,11},{10,... | collective-permute-start | bytes 786440 | tf_op jit(solution)/shard_map/ppermute | solution.py:376
  39.5 24.7 %collective-permute-start.8 = (bf16[2,2,128,256]{3,2,1,0:T(8,128)(2,1)}, bf16[2,2,128,256]{3,2,1,0:T(8,128)(2,1)S(1)}, u32[]{:S(2)}, u32[]{:S(2)}) collective-permute-start(bf16[2,2,128,256]{3,2,1,0:T(8,128)(2,1)} %get-tuple-element.33), channel_id=1, source_target_pairs={{0,3},{1,2},{2,1},{3,0},{4,7},{5,6},{6,5},{7,4},{8,11},{9,10},{10,... | collective-permute-start | bytes 786440 | tf_op jit(solution)/shard_map/ppermute | solution.py:376
  39.6 2.1 %collective-permute-start = (bf16[56,128]{1,0:T(8,128)(2,1)}, bf16[56,128]{1,0:T(8,128)(2,1)S(1)}, u32[]{:S(2)}, u32[]{:S(2)}) collective-permute-start(bf16[56,128]{1,0:T(8,128)(2,1)} %get-tuple-element.26), channel_id=1, source_target_pairs={{0,1},{1,0},{2,3},{3,2},{4,5},{5,4},{6,7},{7,6},{8,9},{9,8},{10,11... | collective-permute-start | bytes 43016 | tf_op jit(solution)/shard_map/ppermute | solution.py:376
  39.7 13.0 %collective-permute-start.1 = (bf16[56,128]{1,0:T(8,128)(2,1)}, bf16[56,128]{1,0:T(8,128)(2,1)S(1)}, u32[]{:S(2)}, u32[]{:S(2)}) collective-permute-start(bf16[56,128]{1,0:T(8,128)(2,1)} %get-tuple-element.27), channel_id=1, source_target_pairs={{0,2},{1,3},{2,0},{3,1},{4,6},{5,7},{6,4},{7,5},{8,10},{9,11},{10,... | collective-permute-start | bytes 43016 | tf_op jit(solution)/shard_map/ppermute | solution.py:376
  41.7 11.0 %collective-permute-start.2 = (bf16[56,128]{1,0:T(8,128)(2,1)}, bf16[56,128]{1,0:T(8,128)(2,1)S(1)}, u32[]{:S(2)}, u32[]{:S(2)}) collective-permute-start(bf16[56,128]{1,0:T(8,128)(2,1)} %get-tuple-element.28), channel_id=1, source_target_pairs={{0,3},{1,2},{2,1},{3,0},{4,7},{5,6},{6,5},{7,4},{8,11},{9,10},{10,... | collective-permute-start | bytes 43016 | tf_op jit(solution)/shard_map/ppermute | solution.py:376
  53.4 10.8 %copy-start.3 = (bf16[224,128]{1,0:T(8,128)(2,1)}, bf16[224,128]{1,0:T(8,128)(2,1)S(1)}, u32[]{:S(2)}) copy-start(bf16[224,128]{1,0:T(8,128)(2,1)S(1)} %pad_maximum_fusion.refs_0_) | copy-start | bytes 172036
  53.4 4.4 %collective-permute-start.3 = (bf16[224,128]{1,0:T(8,128)(2,1)S(1)}, bf16[224,128]{1,0:T(8,128)(2,1)S(1)}, u32[]{:S(2)}, u32[]{:S(2)}) collective-permute-start(bf16[224,128]{1,0:T(8,128)(2,1)S(1)} %pad_maximum_fusion.refs_0_), channel_id=1, source_target_pairs={{0,4},{1,5},{2,6},{3,7},{4,0},{5,1},{6,2},{7,3},{8,12},{9,13},{10,... | collective-permute-start | bytes 172040 | tf_op jit(solution)/shard_map/ppermute | solution.py:376
  55.2 6.8 %collective-permute-start.4 = (bf16[224,128]{1,0:T(8,128)(2,1)S(1)}, bf16[224,128]{1,0:T(8,128)(2,1)S(1)}, u32[]{:S(2)}, u32[]{:S(2)}) collective-permute-start(bf16[224,128]{1,0:T(8,128)(2,1)S(1)} %pad_maximum_fusion.refs_0_), channel_id=1, source_target_pairs={{0,8},{1,9},{2,10},{3,11},{4,12},{5,13},{6,14},{7,15},{8,0},{9,1},... | collective-permute-start | bytes 172040 | tf_op jit(solution)/shard_map/ppermute | solution.py:376
  57.8 6.4 %copy-start.4 = (bf16[224,128]{1,0:T(8,128)(2,1)}, bf16[224,128]{1,0:T(8,128)(2,1)S(1)}, u32[]{:S(2)}) copy-start(bf16[224,128]{1,0:T(8,128)(2,1)S(1)} %collective-permute-done.3.refs_1_) | copy-start | bytes 172036
  57.8 6.4 %collective-permute-start.5 = (bf16[224,128]{1,0:T(8,128)(2,1)S(1)}, bf16[224,128]{1,0:T(8,128)(2,1)S(1)}, u32[]{:S(2)}, u32[]{:S(2)}) collective-permute-start(bf16[224,128]{1,0:T(8,128)(2,1)S(1)} %pad_maximum_fusion.refs_0_), channel_id=1, source_target_pairs={{0,12},{1,13},{2,14},{3,15},{4,8},{5,9},{6,10},{7,11},{8,4},{9,5},... | collective-permute-start | bytes 172040 | tf_op jit(solution)/shard_map/ppermute | solution.py:376
  62.1 2.2 %copy-start.5 = (bf16[224,128]{1,0:T(8,128)(2,1)}, bf16[224,128]{1,0:T(8,128)(2,1)S(1)}, u32[]{:S(2)}) copy-start(bf16[224,128]{1,0:T(8,128)(2,1)S(1)} %collective-permute-done.4.refs_2_) | copy-start | bytes 172036
  64.2 0.6 copy-start.6
  64.2 0.7 copy-start
  64.2 0.8 copy-start.1
  64.2 0.9 copy-start.2
  68.6 5.2 %collective-permute-start.10 = (bf16[208,128]{1,0:T(8,128)(2,1)}, bf16[208,128]{1,0:T(8,128)(2,1)S(1)}, u32[]{:S(2)}, u32[]{:S(2)}) collective-permute-start(bf16[208,128]{1,0:T(8,128)(2,1)} %get-tuple-element.36), channel_id=1, source_target_pairs={{0,8},{1,9},{2,10},{3,11},{4,12},{5,13},{6,14},{7,15},{8,0},{9,1},... | collective-permute-start | bytes 159752 | tf_op jit(solution)/shard_map/ppermute | solution.py:376
  69.5 6.1 %collective-permute-start.11 = (bf16[208,128]{1,0:T(8,128)(2,1)}, bf16[208,128]{1,0:T(8,128)(2,1)S(1)}, u32[]{:S(2)}, u32[]{:S(2)}) collective-permute-start(bf16[208,128]{1,0:T(8,128)(2,1)} %get-tuple-element.37), channel_id=1, source_target_pairs={{0,12},{1,13},{2,14},{3,15},{4,8},{5,9},{6,10},{7,11},{8,4},{9,5},... | collective-permute-start | bytes 159752 | tf_op jit(solution)/shard_map/ppermute | solution.py:376
  72.5 4.3 %collective-permute-start.9 = (bf16[208,128]{1,0:T(8,128)(2,1)}, bf16[208,128]{1,0:T(8,128)(2,1)S(1)}, u32[]{:S(2)}, u32[]{:S(2)}) collective-permute-start(bf16[208,128]{1,0:T(8,128)(2,1)} %get-tuple-element.35), channel_id=1, source_target_pairs={{0,4},{1,5},{2,6},{3,7},{4,0},{5,1},{6,2},{7,3},{8,12},{9,13},{10,... | collective-permute-start | bytes 159752 | tf_op jit(solution)/shard_map/ppermute | solution.py:376
  73.8 3.0 %copy-start.7 = (bf16[208,128]{1,0:T(8,128)(2,1)}, bf16[208,128]{1,0:T(8,128)(2,1)S(1)}, u32[]{:S(2)}) copy-start(bf16[208,128]{1,0:T(8,128)(2,1)S(1)} %collective-permute-done.10.refs_2_) | copy-start | bytes 159748
  75.6 1.2 %copy-start.8 = (bf16[208,128]{1,0:T(8,128)(2,1)}, bf16[208,128]{1,0:T(8,128)(2,1)S(1)}, u32[]{:S(2)}) copy-start(bf16[208,128]{1,0:T(8,128)(2,1)S(1)} %collective-permute-done.11.refs_3_) | copy-start | bytes 159748
  76.8 0.6 copy-start.9
  79.1 7.9 %collective-permute-start.12 = (bf16[64,128]{1,0:T(8,128)(2,1)}, bf16[64,128]{1,0:T(8,128)(2,1)S(1)}, u32[]{:S(2)}, u32[]{:S(2)}) collective-permute-start(bf16[64,128]{1,0:T(8,128)(2,1)} %get-tuple-element.39), channel_id=1, source_target_pairs={{0,1},{1,0},{2,3},{3,2},{4,5},{5,4},{6,7},{7,6},{8,9},{9,8},{10,11... | collective-permute-start | bytes 49160 | tf_op jit(solution)/shard_map/ppermute | solution.py:376
  79.1 7.9 %collective-permute-start.13 = (bf16[64,128]{1,0:T(8,128)(2,1)}, bf16[64,128]{1,0:T(8,128)(2,1)S(1)}, u32[]{:S(2)}, u32[]{:S(2)}) collective-permute-start(bf16[64,128]{1,0:T(8,128)(2,1)} %get-tuple-element.40), channel_id=1, source_target_pairs={{0,2},{1,3},{2,0},{3,1},{4,6},{5,7},{6,4},{7,5},{8,10},{9,11},{10,... | collective-permute-start | bytes 49160 | tf_op jit(solution)/shard_map/ppermute | solution.py:376
  80.7 6.3 %collective-permute-start.14 = (bf16[64,128]{1,0:T(8,128)(2,1)}, bf16[64,128]{1,0:T(8,128)(2,1)S(1)}, u32[]{:S(2)}, u32[]{:S(2)}) collective-permute-start(bf16[64,128]{1,0:T(8,128)(2,1)} %get-tuple-element.41), channel_id=1, source_target_pairs={{0,3},{1,2},{2,1},{3,0},{4,7},{5,6},{6,5},{7,4},{8,11},{9,10},{10,... | collective-permute-start | bytes 49160 | tf_op jit(solution)/shard_map/ppermute | solution.py:376
  87.0 0.6 copy-start.10
  87.0 0.6 copy-start.11
  87.0 0.6 copy-start.12

commit v2 on v1

--- a/solution.py
+++ b/solution.py
@@ -7,6 +7,7 @@
 from jax.experimental.pallas import tpu as pltpu
 from jax.sharding import PartitionSpec as P
 
+
 HD = 128
 BLOCK = 128
 SLAB = 4
@@ -17,6 +18,10 @@
 
 def vmem_spec():
     return pl.BlockSpec(memory_space=pltpu.VMEM)
+
+
+def near(arrays):
+    return [pltpu.with_memory_space_constraint(x, pltpu.VMEM) for x in arrays]
 
 
 def split3(x):
@@ -68,23 +73,12 @@
     def kernel(me_ref, q_ref, ids_ref, cache_ref, all_ref, *rest):
         q_out = rest[:SLAB]
         kv_out = rest[SLAB : 2 * SLAB]
-        scratch, sem = rest[2 * SLAB :]
+        (scratch,) = rest[2 * SLAB :]
         mine = me_ref[0]
-        copies = []
-        for j in range(SLAB):
-            column = pl.multiple_of((mine ^ j) * kvw, kvw)
-            for side in range(2):
-                copy = pltpu.make_async_copy(
-                    cache_ref.at[:, :, pl.ds(side * kv_width + column, kvw)],
-                    kv_out[j].at[side],
-                    sem.at[j, side],
-                )
-                copy.start()
-                copies.append(copy)
         for h in range(heads):
             scratch[pl.ds(h, cands, stride=heads), :] = q_ref[:, h * HD : (h + 1) * HD].astype(F32)
         all_ref[...] = scratch[...].astype(BF16)
-        id_rows = [jnp.full((1, HD), ids_ref[r, 0].astype(F32)) for r in range(cands)]
+        id_rows = [jnp.full((1, HD), ids_ref[r].astype(F32)) for r in range(cands)]
         id_rows = id_rows + [jnp.zeros((8 - cands, HD), F32)]
         for j in range(SLAB):
             first = (mine ^ j) * hq
@@ -94,53 +88,63 @@
                     at = pl.multiple_of(r * heads + first + k * group, 8)
                     pieces.append(scratch[pl.ds(at, group), :])
             q_out[j][...] = jnp.concatenate(pieces + id_rows, axis=0).astype(BF16)
-        for copy in copies:
-            copy.wait()
+        for j in range(SLAB):
+            for side in range(2):
+                column = pl.multiple_of(side * kv_width + (mine ^ j) * kvw, kvw)
+                kv_out[j][side] = cache_ref[:, :, pl.ds(column, kvw)]
 
     smem = pl.BlockSpec(memory_space=pltpu.SMEM)
-    hbm = pl.BlockSpec(memory_space=pl.ANY)
     out = pl.pallas_call(
         kernel,
-        out_shape=[jax.ShapeDtypeStruct((cands * heads, HD), BF16)]
-        + [jax.ShapeDtypeStruct((part_rows, HD), BF16)] * SLAB
-        + [jax.ShapeDtypeStruct((2, prompts, span, kvw), BF16)] * SLAB,
-        in_specs=[smem, vmem_spec(), smem, hbm],
-        out_specs=[vmem_spec()] * (1 + SLAB) + [hbm] * SLAB,
+        out_shape=[pltpu.VMEM((cands * heads, HD), BF16)]
+        + [pltpu.VMEM((part_rows, HD), BF16)] * SLAB
+        + [pltpu.VMEM((2, prompts, span, kvw), BF16)] * SLAB,
+        in_specs=[smem, vmem_spec(), smem, vmem_spec()],
+        out_specs=[vmem_spec()] * (1 + 2 * SLAB),
         scratch_shapes=[
             pltpu.VMEM((cands * heads, HD), F32),
-            pltpu.SemaphoreType.DMA((SLAB, 2)),
         ],
         name="prepare",
     )(me, queries, prompt_of, prompt_cache)
     return out[0], out[1 : 1 + SLAB], out[1 + SLAB :]
 
 
-def suffix_attend(blocks, rows_q, suffix_cache, kv_heads):
+def suffix_attend(which, blocks, rows_q, suffix_cache, kv_heads):
     cands, length, kv_width2 = suffix_cache.shape
     kv_width = kv_width2 // 2
     heads = rows_q.shape[0] // cands
     group = heads // kv_heads
 
-    def kernel(blocks_ref, q_ref, key_ref, value_ref, max_ref, sum_ref, mix_ref):
-        q = q_ref[...]
+    def kernel(blocks_ref, q_ref, cache_ref, max_ref, sum_ref, mix_ref, keys, values, sem):
+        fetches = [
+            pltpu.make_async_copy(
+                cache_ref.at[which, :, side * kv_width : (side + 1) * kv_width], target, sem.at[side]
+            )
+            for side, target in enumerate((keys, values))
+        ]
+        for fetch in fetches:
+            fetch.start()
+        q = q_ref[which * heads : (which + 1) * heads, :]
         wide = jnp.concatenate([q] * kv_heads, axis=1)
         diagonal = (
             lax.broadcasted_iota(jnp.int32, (heads, kv_width), 0) // group
             == lax.broadcasted_iota(jnp.int32, (heads, kv_width), 1) // HD
         )
         wide = jnp.where(diagonal, wide, jnp.zeros_like(wide))
+        fetches[0].wait()
         logits = lax.dot_general(
-            wide, key_ref[0], (((1,), (1,)), ((), ())), preferred_element_type=F32
+            wide,
+            keys[...],
+            (((1,), (1,)), ((), ())),
+            preferred_element_type=F32,
         ) * HD ** (-0.5)
-        live = (
-            lax.broadcasted_iota(jnp.int32, (heads, length), 1)
-            < BLOCK * blocks_ref[pl.program_id(0)]
-        )
+        live = lax.broadcasted_iota(jnp.int32, (heads, length), 1) < BLOCK * blocks_ref[which]
         logits = jnp.where(live, logits, floor_logit)
         maxima = jnp.max(logits, axis=1, keepdims=True)
         exponent = jnp.where(live, jnp.exp(logits - maxima), 0.0)
         totals = jnp.sum(exponent, axis=1, keepdims=True)
-        mixed = jnp.dot(exponent.astype(BF16), value_ref[0], preferred_element_type=F32)
+        fetches[1].wait()
+        mixed = jnp.dot(exponent.astype(BF16), values[...], preferred_element_type=F32)
         max_ref[...] = jnp.broadcast_to(maxima, (heads, HD))
         sum_ref[...] = jnp.broadcast_to(totals, (heads, HD))
         for k in range(kv_heads):
@@ -148,28 +152,27 @@
                 k * group : (k + 1) * group, k * HD : (k + 1) * HD
             ]
 
-    shape = jax.ShapeDtypeStruct((cands * heads, HD), F32)
-    row_spec = pl.BlockSpec((heads, HD), lambda c, b: (c, 0))
     return pl.pallas_call(
         kernel,
-        out_shape=[shape] * 3,
-        grid_spec=pltpu.PrefetchScalarGridSpec(
-            num_scalar_prefetch=1,
-            grid=(cands,),
-            in_specs=[
-                row_spec,
-                pl.BlockSpec((1, length, kv_width), lambda c, b: (c, 0, 0)),
-                pl.BlockSpec((1, length, kv_width), lambda c, b: (c, 0, 1)),
-            ],
-            out_specs=[row_spec] * 3,
-        ),
+        out_shape=[pltpu.VMEM((heads, HD), F32)] * 3,
+        in_specs=[
+            pl.BlockSpec(memory_space=pltpu.SMEM),
+            vmem_spec(),
+            pl.BlockSpec(memory_space=pl.ANY),
+        ],
+        out_specs=[vmem_spec()] * 3,
+        scratch_shapes=[
+            pltpu.VMEM((length, kv_width), BF16),
+            pltpu.VMEM((length, kv_width), BF16),
+            pltpu.SemaphoreType.DMA((2,)),
+        ],
         cost_estimate=pl.CostEstimate(
-            flops=4 * cands * heads * length * kv_width,
-            transcendentals=cands * heads * length,
-            bytes_accessed=2 * suffix_cache.size,
+            flops=4 * heads * length * kv_width,
+            transcendentals=heads * length,
+            bytes_accessed=2 * suffix_cache.size // cands,
         ),
         name="suffix",
-    )(blocks, rows_q, suffix_cache, suffix_cache)
+    )(blocks, *near([rows_q]), suffix_cache)
 
 
 def prompt_attend(query_blocks, caches, cands, kvq, group):
@@ -202,7 +205,7 @@
         ids = jnp.concatenate(ids, axis=0)
         ids = jnp.concatenate([ids] * (width // HD), axis=1)
         picked = [ids == float(p) for p in range(prompts)]
-        stats = [[] for i in range(chunk)]
+        stats = [[] for _ in range(chunk)]
         for k in range(kvq):
             q = jnp.concatenate(
                 [
@@ -254,11 +257,11 @@
         )(query_blocks, *caches)
     return pl.pallas_call(
         kernel,
-        out_shape=[jax.ShapeDtypeStruct((out_rows, HD), BF16)] * outer,
+        out_shape=[pltpu.VMEM((out_rows, HD), BF16)] * outer,
         in_specs=[vmem_spec()] * (outer + SLAB),
         out_specs=[vmem_spec()] * outer,
         name="prompt",
-    )(*query_blocks, *caches)
+    )(*near(query_blocks), *near(caches))
 
 
 def merge(blocks, cands, kvq, group):
@@ -302,11 +305,11 @@
     args = [blocks] if stacked else blocks
     return pl.pallas_call(
         kernel,
-        out_shape=[jax.ShapeDtypeStruct((out_rows, HD), BF16)] * SLAB,
+        out_shape=[pltpu.VMEM((out_rows, HD), BF16)] * SLAB,
         in_specs=[vmem_spec()] * len(args),
         out_specs=[vmem_spec()] * SLAB,
         name="merge",
-    )(*args)
+    )(*near(args))
 
 
 def finish(me, pieces, suffix_state, reward, cands, kvq, group):
@@ -316,9 +319,10 @@
 
     def kernel(me_ref, *refs):
         piece_refs = refs[:SLAB]
-        max_ref, sum_ref, mix_ref, reward_ref, out_ref, score_ref, scratch = refs[SLAB:]
+        state_refs = refs[SLAB : SLAB + 3 * cands]
+        reward_ref, out_ref, score_ref, scratch = refs[SLAB + 3 * cands :]
         mine = me_ref[0]
-        scores = [jnp.zeros((group, HD), F32) for r in range(cands)]
+        scores = [jnp.zeros((group, HD), F32) for _ in range(cands)]
         for j in range(SLAB):
             first = (mine ^ j) * hq
             stats = piece_refs[j][kvq * part :, :].astype(F32)
@@ -329,7 +333,9 @@
                 total = to_rows(total, part, j * part)
                 weight = reward_ref[pl.ds(pl.multiple_of(first + k * group, 8), group), :]
                 for r in range(cands):
-                    at = pl.ds(pl.multiple_of(r * heads + first + k * group, 8), group)
+                    max_ref, sum_ref, mix_ref = state_refs[3 * r : 3 * r + 3]
+                    at = pl.ds(pl.multiple_of(first + k * group, 8), group)
+                    row = pl.ds(pl.multiple_of(r * heads + first + k * group, 8), group)
                     cut = slice(r * group, (r + 1) * group)
                     home_max = max_ref[at, :]
                     here_max = jnp.broadcast_to(maximum[cut], (group, HD))
@@ -339,7 +345,7 @@
                     total_all = home * sum_ref[at, :] + here * total[cut]
                     mixed = home * mix_ref[at, :] + here * mix[k * part :][cut]
                     attended = (mixed / total_all).astype(BF16).astype(F32)
-                    scratch[at, :] = attended
+                    scratch[row, :] = attended
                     scores[r] = scores[r] + attended * weight
         for h in range(heads):
             out_ref[:, h * HD : (h + 1) * HD] = scratch[pl.ds(h, cands, stride=heads), :].astype(
@@ -355,14 +361,14 @@
             jax.ShapeDtypeStruct((cands, heads * HD), BF16),
             jax.ShapeDtypeStruct((cands,), F32),
         ],
-        in_specs=[smem] + [vmem_spec()] * (SLAB + 4),
+        in_specs=[smem] + [vmem_spec()] * (SLAB + 3 * cands + 1),
         out_specs=[vmem_spec(), smem],
         scratch_shapes=[pltpu.VMEM((cands * heads, HD), F32)],
         name="finish",
-    )(me, *pieces, *suffix_state, reward)
-
-
-def body(queries, prompt_of, suffix_cache, suffix_blocks, prompt_cache, reward_weight):
+    )(me, *near(pieces), *near(suffix_state), reward)
+
+
+def attend(queries, prompt_of, suffix_cache, suffix_blocks, prompt_cache, reward_weight):
     cands = queries.shape[0]
     heads = queries.shape[1] // HD
     kv_heads = prompt_cache.shape[2] // (2 * HD)
@@ -375,30 +381,38 @@
     def hop(x, step):
         return lax.ppermute(x, "seq", [(i, i ^ step) for i in range(devices)])
 
-    direct = outer <= 4 and outer & (outer - 1) == 0
+    def spread(arrays, step):
+        return [arrays[0]] + [hop(arrays[i], step * i) for i in range(1, len(arrays))]
+
+    direct = is_direct(devices)
     columns = [[SLAB * z + i for z in range(outer)] for i in range(SLAB)]
 
-    rows_q, q_parts, kv_parts = prepare(me, queries, prompt_of, prompt_cache, kvq, group)
-    q_parts = [q_parts[0]] + [hop(q_parts[j], j) for j in range(1, SLAB)]
-    kv_parts = [kv_parts[0]] + [hop(kv_parts[j], j) for j in range(1, SLAB)]
+    rows_q, q_parts, kv_parts = prepare(me, queries, prompt_of[:, 0], prompt_cache, kvq, group)
+    q_parts = spread(q_parts, 1)
+    kv_parts = spread(kv_parts, 1)
     q_slab = jnp.concatenate(q_parts, axis=0)
-    rows_q, q_slab = lax.optimization_barrier((rows_q, q_slab))
-    suffix_state = suffix_attend(suffix_blocks, rows_q, suffix_cache, kv_heads)
+    suffix_state = []
+    for c in range(cands):
+        suffix_state += suffix_attend(c, suffix_blocks, rows_q, suffix_cache, kv_heads)
     if direct:
-        q_all = [q_slab] + [hop(q_slab, SLAB * i) for i in range(1, outer)]
+        q_all = spread([q_slab] * outer, SLAB)
     else:
         q_all = lax.all_gather(q_slab, "seq", axis_index_groups=columns)
     partial = prompt_attend(q_all, kv_parts, cands, kvq, group)
     if direct:
-        partial = [partial[0]] + [hop(partial[i], SLAB * i) for i in range(1, outer)]
+        partial = spread(partial, SLAB)
     else:
         partial = lax.all_to_all(
             partial, "seq", split_axis=0, concat_axis=0, axis_index_groups=columns, tiled=True
         )
-    pieces = merge(partial, cands, kvq, group)
-    pieces = [pieces[0]] + [hop(pieces[j], j) for j in range(1, SLAB)]
+    pieces = spread(merge(partial, cands, kvq, group), 1)
     reward = reward_weight.reshape(heads, HD)
     return tuple(finish(me, pieces, suffix_state, reward, cands, kvq, group))
+
+
+def is_direct(devices):
+    outer = devices // SLAB
+    return outer == 4
 
 
 def solution(mesh):
@@ -411,7 +425,7 @@
         P(),
     )
     return jax.shard_map(
-        body,
+        attend,
         mesh=mesh,
         in_specs=placed,
         out_specs=(P(("groups", "seq"), None), P(("groups", "seq"))),

time: 89.9 us -> 39.7 us (0.44)
  Pallas kernels: 47.5 us -> 13.3 us
  waiting for transfers between devices: 16 us -> 5.54 us
  local copies, waits for them, and re-layouts: 3.38 us -> 0.03 us
  starting transfers between devices: 21.1 us -> 19.7 us
    pallas_call x4 -> x6, Pallas kernels: 45.6 us -> 11.7 us  [the longest x3 8.44 us: suffix_attend(): pl.pallas_call(kernel, out_shape=[pltpu.VMEM((heads, HD), F32)] * 3, in_s...]
    ppermute x15, waiting for transfers between devices: 16 us -> 5.54 us  [hop(): return lax.ppermute(x, 'seq', [(i, i ^ step) for i in range(devices)])]
    unnamed x27 -> x3, local copies, waits for them, and re-layouts: 3.38 us -> 0.02 us
    ppermute x15, starting transfers between devices: 21.1 us -> 19.7 us  [hop(): return lax.ppermute(x, 'seq', [(i, i ^ step) for i in range(devices)])]
  transfers between devices with their start and end apart: 15 -> 15, of which waited for: 5 -> 5; matrix products, arithmetic and copies ran while one was open for 1% -> 0% of each run, Pallas kernels for 7% -> 21%
where the time goes in v2:
time: 39.7 us; the launch traced here: 39.4 us
  starting transfers between devices  19.7 us (50%)
  Pallas kernels  13.3 us (34%)
  waiting for transfers between devices  5.54 us (14%)
  between operations  0.76 us (2%)
    ppermute x15, starting transfers between devices, hop(): return lax.ppermute(x, 'seq', [(i, i ^ step) for i in range(devices)])  19.7 us
    pallas_call x3, Pallas kernels, suffix_attend(): pl.pallas_call(kernel, out_shape=[pltpu.VMEM((heads, HD), F32)] * 3, in_s...  8.44 us
    ppermute x15, waiting for transfers between devices, hop(): return lax.ppermute(x, 'seq', [(i, i ^ step) for i in range(devices)])  5.54 us
    pallas_call x1, Pallas kernels, finish(): pl.pallas_call(kernel, out_shape=[jax.ShapeDtypeStruct((cands, heads * HD...  1.64 us
    pallas_call x1, Pallas kernels, prompt_attend(): pl.pallas_call(kernel, out_shape=[pltpu.VMEM((out_rows, HD), BF16)] * out...  1.53 us
    pallas_call x1, Pallas kernels, prepare(): pl.pallas_call(kernel, out_shape=[pltpu.VMEM((cands * heads, HD), BF16)]...  1.49 us
  transfers between devices with their start and end apart: 15, of which 5 were waited for; matrix products, arithmetic and copies ran while one was open for 0% of the time, Pallas kernels for 21%

profile of v2, /device:TPU:0, one launch (start us, length us, event | category | flops | bytes accessed | tf_op | source)
XLA Modules:
  0.0 39.4 jit_solution(7232639335628206339)
XLA Ops:
  0.6 1.5 %prepare.1 = (bf16[192,128]{1,0:T(8,128)(2,1)S(1)}, bf16[56,128]{1,0:T(8,128)(2,1)S(1)}, bf16[56,128]{1,0:T(8,128)(2,1)S(1)}, bf16[56,128]{1,0:T(8,128)(2,1)S(1)...) custom-call(s32[1]{0:T(128)} %bitcast.me_ref, ...), custom_call_target="tpu_custom_call" | custom-call | tf_op jit(solution)/shard_map/prepare/pallas_call | solution.py:97
  2.1 0.6 %collective-permute-start = (bf16[56,128]{1,0:T(8,128)(2,1)S(1)}, bf16[56,128]{1,0:T(8,128)(2,1)S(1)}, u32[]{:S(2)}, u32[]{:S(2)}) collective-permute-start(bf16[56,128]{1,0:T(8,128)(2,1)S(1)} %get-tuple-element.29), channel_id=1, source_target_pairs={{0,1},{1,0},{2,3},{3,2},{4,5},{5,4},{6,7},{7,6},{8,9},{9,8},{10,11... | collective-permute-start | bytes 43016 | tf_op jit(solution)/shard_map/ppermute | solution.py:382
  2.7 2.6 %collective-permute-start.1 = (bf16[56,128]{1,0:T(8,128)(2,1)S(1)}, bf16[56,128]{1,0:T(8,128)(2,1)S(1)}, u32[]{:S(2)}, u32[]{:S(2)}) collective-permute-start(bf16[56,128]{1,0:T(8,128)(2,1)S(1)} %get-tuple-element.30), channel_id=1, source_target_pairs={{0,2},{1,3},{2,0},{3,1},{4,6},{5,7},{6,4},{7,5},{8,10},{9,11},{10,... | collective-permute-start | bytes 43016 | tf_op jit(solution)/shard_map/ppermute | solution.py:382
  5.3 0.0 collective-permute-start.2
  5.3 0.2 collective-permute-start.6
  5.5 1.9 %collective-permute-start.7 = (bf16[2,2,128,256]{3,2,1,0:T(8,128)(2,1)S(1)}, bf16[2,2,128,256]{3,2,1,0:T(8,128)(2,1)S(1)}, u32[]{:S(2)}, u32[]{:S(2)}) collective-permute-start(bf16[2,2,128,256]{3,2,1,0:T(8,128)(2,1)S(1)} %get-tuple-element.34), channel_id=1, source_target_pairs={{0,2},{1,3},{2,0},{3,1},{4,6},{5,7},{6,4},{7,5},{8,10},{9,11},{10,... | collective-permute-start | bytes 786440 | tf_op jit(solution)/shard_map/ppermute | solution.py:382
  7.4 0.0 collective-permute-done
  7.4 0.0 collective-permute-start.8
  7.4 0.0 collective-permute-done.1
  7.5 1.0 %collective-permute-done.2 = bf16[56,128]{1,0:T(8,128)(2,1)S(1)} collective-permute-done((bf16[56,128]{1,0:T(8,128)(2,1)S(1)}, bf16[56,128]{1,0:T(8,128)(2,1)S(1)}, u32[]{:S(2)}, u32[]{:S(2)}) %collective-permute-start.2) | collective-permute-done | bytes 14368 | tf_op jit(solution)/shard_map/ppermute | solution.py:382
  8.4 1.6 %collective-permute-start.3 = (bf16[224,128]{1,0:T(8,128)(2,1)S(1)}, bf16[224,128]{1,0:T(8,128)(2,1)S(1)}, u32[]{:S(2)}, u32[]{:S(2)}) collective-permute-start(bf16[224,128]{1,0:T(8,128)(2,1)S(1)} %constant_dynamic-update-slice_fusion.refs_0_), channel_id=1, source_target_pairs={{0,4},{1,5},{2,6},{3,7},{4,0},{5,1},{6,2},{7,3},{8,12},{9,13},{10,... | collective-permute-start | bytes 172040 | tf_op jit(solution)/shard_map/ppermute | solution.py:382
  10.0 2.6 %collective-permute-start.4 = (bf16[224,128]{1,0:T(8,128)(2,1)S(1)}, bf16[224,128]{1,0:T(8,128)(2,1)S(1)}, u32[]{:S(2)}, u32[]{:S(2)}) collective-permute-start(bf16[224,128]{1,0:T(8,128)(2,1)S(1)} %constant_dynamic-update-slice_fusion.refs_0_), channel_id=1, source_target_pairs={{0,8},{1,9},{2,10},{3,11},{4,12},{5,13},{6,14},{7,15},{8,0},{9,1},... | collective-permute-start | bytes 172040 | tf_op jit(solution)/shard_map/ppermute | solution.py:382
  12.6 0.0 collective-permute-done.3.refs_1_
  12.6 4.2 %collective-permute-start.5 = (bf16[224,128]{1,0:T(8,128)(2,1)S(1)}, bf16[224,128]{1,0:T(8,128)(2,1)S(1)}, u32[]{:S(2)}, u32[]{:S(2)}) collective-permute-start(bf16[224,128]{1,0:T(8,128)(2,1)S(1)} %constant_dynamic-update-slice_fusion.refs_0_), channel_id=1, source_target_pairs={{0,12},{1,13},{2,14},{3,15},{4,8},{5,9},{6,10},{7,11},{8,4},{9,5},... | collective-permute-start | bytes 172040 | tf_op jit(solution)/shard_map/ppermute | solution.py:382
  16.8 0.0 collective-permute-done.4.refs_2_
  16.8 2.2 %collective-permute-done.5.refs_3_ = bf16[224,128]{1,0:T(8,128)(2,1)S(1)} collective-permute-done((bf16[224,128]{1,0:T(8,128)(2,1)S(1)}, bf16[224,128]{1,0:T(8,128)(2,1)S(1)}, u32[]{:S(2)}, u32[]{:S(2)}) %collective-permute-start.5) | collective-permute-done | bytes 57376 | tf_op jit(solution)/shard_map/ppermute | solution.py:382
  19.0 0.0 collective-permute-done.6.refs_5_
  19.0 0.0 collective-permute-done.7.refs_6_
  19.0 0.4 collective-permute-done.8.refs_7_
  19.3 1.5 %prompt.1 = (bf16[208,128]{1,0:T(8,128)(2,1)S(1)}, bf16[208,128]{1,0:T(8,128)(2,1)S(1)}, bf16[208,128]{1,0:T(8,128)(2,1)S(1)}, bf16[208,128]{1,0:T(8,128)(2,1)S(1)}) custom-call(bf16[224,128]{1,0:T(8,128)(2,1)S(1)} %constant_dynamic-update-slice_fusion.refs_0_, bf16[224,128]{1,0:T(8,128)(2,1)S(1)} %collective-permute-done.3.refs_1_, ...), custom_call_target="tpu_custom_call" | custom-call | tf_op jit(solution)/shard_map/prompt/pallas_call | solution.py:258
  20.9 2.6 %collective-permute-start.10 = (bf16[208,128]{1,0:T(8,128)(2,1)S(1)}, bf16[208,128]{1,0:T(8,128)(2,1)S(1)}, u32[]{:S(2)}, u32[]{:S(2)}) collective-permute-start(bf16[208,128]{1,0:T(8,128)(2,1)S(1)} %get-tuple-element.38), channel_id=1, source_target_pairs={{0,8},{1,9},{2,10},{3,11},{4,12},{5,13},{6,14},{7,15},{8,0},{9,1},... | collective-permute-start | bytes 159752 | tf_op jit(solution)/shard_map/ppermute | solution.py:382
  23.5 1.3 %collective-permute-start.11 = (bf16[208,128]{1,0:T(8,128)(2,1)S(1)}, bf16[208,128]{1,0:T(8,128)(2,1)S(1)}, u32[]{:S(2)}, u32[]{:S(2)}) collective-permute-start(bf16[208,128]{1,0:T(8,128)(2,1)S(1)} %get-tuple-element.39), channel_id=1, source_target_pairs={{0,12},{1,13},{2,14},{3,15},{4,8},{5,9},{6,10},{7,11},{8,4},{9,5},... | collective-permute-start | bytes 159752 | tf_op jit(solution)/shard_map/ppermute | solution.py:382
  24.8 0.2 collective-permute-start.9
  25.0 2.8 %suffix.3 = (f32[64,128]{1,0:T(8,128)S(1)}, f32[64,128]{1,0:T(8,128)S(1)}, f32[64,128]{1,0:T(8,128)S(1)}) custom-call(s32[3]{0:T(128)} %blocks_ref.5, bf16[192,128]{1,0:T(8,128)(2,1)S(1)} %get-tuple-element.44.q_ref, bf16[3,512,2048]{2,1,0:T(8,128)(2,1)} %cache_ref.7), custom_call_target="tpu_custom_call" | custom-call | flops 134217728 | bytes 2097152 | tf_op jit(solution)/shard_map/suffix/pallas_call | solution.py:155
  27.9 0.0 collective-permute-done.10.refs_2_
  27.9 1.9 %collective-permute-done.11.refs_3_ = bf16[208,128]{1,0:T(8,128)(2,1)S(1)} collective-permute-done((bf16[208,128]{1,0:T(8,128)(2,1)S(1)}, bf16[208,128]{1,0:T(8,128)(2,1)S(1)}, u32[]{:S(2)}, u32[]{:S(2)}) %collective-permute-start.11) | collective-permute-done | bytes 53280 | tf_op jit(solution)/shard_map/ppermute | solution.py:382
  29.8 0.1 collective-permute-done.9.refs_1_
  29.9 0.2 merge.1
  30.1 0.1 collective-permute-start.12
  30.2 1.5 %collective-permute-start.13 = (bf16[64,128]{1,0:T(8,128)(2,1)S(1)}, bf16[64,128]{1,0:T(8,128)(2,1)S(1)}, u32[]{:S(2)}, u32[]{:S(2)}) collective-permute-start(bf16[64,128]{1,0:T(8,128)(2,1)S(1)} %get-tuple-element.42), channel_id=1, source_target_pairs={{0,2},{1,3},{2,0},{3,1},{4,6},{5,7},{6,4},{7,5},{8,10},{9,11},{10,... | collective-permute-start | bytes 49160 | tf_op jit(solution)/shard_map/ppermute | solution.py:382
  31.7 0.4 collective-permute-start.14
  32.0 2.8 %suffix.4 = (f32[64,128]{1,0:T(8,128)S(1)}, f32[64,128]{1,0:T(8,128)S(1)}, f32[64,128]{1,0:T(8,128)S(1)}) custom-call(s32[3]{0:T(128)} %blocks_ref.5, bf16[192,128]{1,0:T(8,128)(2,1)S(1)} %get-tuple-element.44.q_ref, bf16[3,512,2048]{2,1,0:T(8,128)(2,1)} %cache_ref.7), custom_call_target="tpu_custom_call" | custom-call | flops 134217728 | bytes 2097152 | tf_op jit(solution)/shard_map/suffix/pallas_call | solution.py:155
  34.9 2.8 %suffix.5 = (f32[64,128]{1,0:T(8,128)S(1)}, f32[64,128]{1,0:T(8,128)S(1)}, f32[64,128]{1,0:T(8,128)S(1)}) custom-call(s32[3]{0:T(128)} %blocks_ref.5, bf16[192,128]{1,0:T(8,128)(2,1)S(1)} %get-tuple-element.44.q_ref, bf16[3,512,2048]{2,1,0:T(8,128)(2,1)} %cache_ref.7), custom_call_target="tpu_custom_call" | custom-call | flops 134217728 | bytes 2097152 | tf_op jit(solution)/shard_map/suffix/pallas_call | solution.py:155
  37.7 0.0 collective-permute-done.12.refs_1_
  37.7 0.0 collective-permute-done.13.refs_2_
  37.7 0.0 collective-permute-done.14.refs_3_
  37.7 1.6 %finish.1 = (bf16[3,8192]{1,0:T(4,128)(2,1)}, f32[3]{0:T(128)}) custom-call(s32[1]{0:T(128)} %bitcast.me_ref, bf16[64,128]{1,0:T(8,128)(2,1)S(1)} %get-tuple-element.40.refs_0_, bf16[64,128]{1,0:T(8,128)(2,1)S(1)} %collective-permute-done.12.refs_1_, bf16[64,128]{1,0:T(8,128)(2,1)S(1)} %collective-permute-done.13.refs_2_, ...), custom_call_target="tpu_custom_call" | custom-call | tf_op jit(solution)/shard_map/finish/pallas_call | solution.py:358
  (4 shorter events, 0.0 us)
Async XLA Ops:
  2.1 5.3 %collective-permute-start = (bf16[56,128]{1,0:T(8,128)(2,1)S(1)}, bf16[56,128]{1,0:T(8,128)(2,1)S(1)}, u32[]{:S(2)}, u32[]{:S(2)}) collective-permute-start(bf16[56,128]{1,0:T(8,128)(2,1)S(1)} %get-tuple-element.29), channel_id=1, source_target_pairs={{0,1},{1,0},{2,3},{3,2},{4,5},{5,4},{6,7},{7,6},{8,9},{9,8},{10,11... | collective-permute-start | bytes 43016 | tf_op jit(solution)/shard_map/ppermute | solution.py:382
  2.7 4.8 %collective-permute-start.1 = (bf16[56,128]{1,0:T(8,128)(2,1)S(1)}, bf16[56,128]{1,0:T(8,128)(2,1)S(1)}, u32[]{:S(2)}, u32[]{:S(2)}) collective-permute-start(bf16[56,128]{1,0:T(8,128)(2,1)S(1)} %get-tuple-element.30), channel_id=1, source_target_pairs={{0,2},{1,3},{2,0},{3,1},{4,6},{5,7},{6,4},{7,5},{8,10},{9,11},{10,... | collective-permute-start | bytes 43016 | tf_op jit(solution)/shard_map/ppermute | solution.py:382
  5.3 3.1 %collective-permute-start.2 = (bf16[56,128]{1,0:T(8,128)(2,1)S(1)}, bf16[56,128]{1,0:T(8,128)(2,1)S(1)}, u32[]{:S(2)}, u32[]{:S(2)}) collective-permute-start(bf16[56,128]{1,0:T(8,128)(2,1)S(1)} %get-tuple-element.31), channel_id=1, source_target_pairs={{0,3},{1,2},{2,1},{3,0},{4,7},{5,6},{6,5},{7,4},{8,11},{9,10},{10,... | collective-permute-start | bytes 43016 | tf_op jit(solution)/shard_map/ppermute | solution.py:382
  5.3 13.7 %collective-permute-start.6 = (bf16[2,2,128,256]{3,2,1,0:T(8,128)(2,1)S(1)}, bf16[2,2,128,256]{3,2,1,0:T(8,128)(2,1)S(1)}, u32[]{:S(2)}, u32[]{:S(2)}) collective-permute-start(bf16[2,2,128,256]{3,2,1,0:T(8,128)(2,1)S(1)} %get-tuple-element.33), channel_id=1, source_target_pairs={{0,1},{1,0},{2,3},{3,2},{4,5},{5,4},{6,7},{7,6},{8,9},{9,8},{10,11... | collective-permute-start | bytes 786440 | tf_op jit(solution)/shard_map/ppermute | solution.py:382
  5.5 13.5 %collective-permute-start.7 = (bf16[2,2,128,256]{3,2,1,0:T(8,128)(2,1)S(1)}, bf16[2,2,128,256]{3,2,1,0:T(8,128)(2,1)S(1)}, u32[]{:S(2)}, u32[]{:S(2)}) collective-permute-start(bf16[2,2,128,256]{3,2,1,0:T(8,128)(2,1)S(1)} %get-tuple-element.34), channel_id=1, source_target_pairs={{0,2},{1,3},{2,0},{3,1},{4,6},{5,7},{6,4},{7,5},{8,10},{9,11},{10,... | collective-permute-start | bytes 786440 | tf_op jit(solution)/shard_map/ppermute | solution.py:382
  7.4 11.9 %collective-permute-start.8 = (bf16[2,2,128,256]{3,2,1,0:T(8,128)(2,1)S(1)}, bf16[2,2,128,256]{3,2,1,0:T(8,128)(2,1)S(1)}, u32[]{:S(2)}, u32[]{:S(2)}) collective-permute-start(bf16[2,2,128,256]{3,2,1,0:T(8,128)(2,1)S(1)} %get-tuple-element.35), channel_id=1, source_target_pairs={{0,3},{1,2},{2,1},{3,0},{4,7},{5,6},{6,5},{7,4},{8,11},{9,10},{10,... | collective-permute-start | bytes 786440 | tf_op jit(solution)/shard_map/ppermute | solution.py:382
  8.4 4.2 %collective-permute-start.3 = (bf16[224,128]{1,0:T(8,128)(2,1)S(1)}, bf16[224,128]{1,0:T(8,128)(2,1)S(1)}, u32[]{:S(2)}, u32[]{:S(2)}) collective-permute-start(bf16[224,128]{1,0:T(8,128)(2,1)S(1)} %constant_dynamic-update-slice_fusion.refs_0_), channel_id=1, source_target_pairs={{0,4},{1,5},{2,6},{3,7},{4,0},{5,1},{6,2},{7,3},{8,12},{9,13},{10,... | collective-permute-start | bytes 172040 | tf_op jit(solution)/shard_map/ppermute | solution.py:382
  10.0 6.8 %collective-permute-start.4 = (bf16[224,128]{1,0:T(8,128)(2,1)S(1)}, bf16[224,128]{1,0:T(8,128)(2,1)S(1)}, u32[]{:S(2)}, u32[]{:S(2)}) collective-permute-start(bf16[224,128]{1,0:T(8,128)(2,1)S(1)} %constant_dynamic-update-slice_fusion.refs_0_), channel_id=1, source_target_pairs={{0,8},{1,9},{2,10},{3,11},{4,12},{5,13},{6,14},{7,15},{8,0},{9,1},... | collective-permute-start | bytes 172040 | tf_op jit(solution)/shard_map/ppermute | solution.py:382
  12.6 6.4 %collective-permute-start.5 = (bf16[224,128]{1,0:T(8,128)(2,1)S(1)}, bf16[224,128]{1,0:T(8,128)(2,1)S(1)}, u32[]{:S(2)}, u32[]{:S(2)}) collective-permute-start(bf16[224,128]{1,0:T(8,128)(2,1)S(1)} %constant_dynamic-update-slice_fusion.refs_0_), channel_id=1, source_target_pairs={{0,12},{1,13},{2,14},{3,15},{4,8},{5,9},{6,10},{7,11},{8,4},{9,5},... | collective-permute-start | bytes 172040 | tf_op jit(solution)/shard_map/ppermute | solution.py:382
  20.9 7.0 %collective-permute-start.10 = (bf16[208,128]{1,0:T(8,128)(2,1)S(1)}, bf16[208,128]{1,0:T(8,128)(2,1)S(1)}, u32[]{:S(2)}, u32[]{:S(2)}) collective-permute-start(bf16[208,128]{1,0:T(8,128)(2,1)S(1)} %get-tuple-element.38), channel_id=1, source_target_pairs={{0,8},{1,9},{2,10},{3,11},{4,12},{5,13},{6,14},{7,15},{8,0},{9,1},... | collective-permute-start | bytes 159752 | tf_op jit(solution)/shard_map/ppermute | solution.py:382
  23.5 6.4 %collective-permute-start.11 = (bf16[208,128]{1,0:T(8,128)(2,1)S(1)}, bf16[208,128]{1,0:T(8,128)(2,1)S(1)}, u32[]{:S(2)}, u32[]{:S(2)}) collective-permute-start(bf16[208,128]{1,0:T(8,128)(2,1)S(1)} %get-tuple-element.39), channel_id=1, source_target_pairs={{0,12},{1,13},{2,14},{3,15},{4,8},{5,9},{6,10},{7,11},{8,4},{9,5},... | collective-permute-start | bytes 159752 | tf_op jit(solution)/shard_map/ppermute | solution.py:382
  24.8 5.1 %collective-permute-start.9 = (bf16[208,128]{1,0:T(8,128)(2,1)S(1)}, bf16[208,128]{1,0:T(8,128)(2,1)S(1)}, u32[]{:S(2)}, u32[]{:S(2)}) collective-permute-start(bf16[208,128]{1,0:T(8,128)(2,1)S(1)} %get-tuple-element.37), channel_id=1, source_target_pairs={{0,4},{1,5},{2,6},{3,7},{4,0},{5,1},{6,2},{7,3},{8,12},{9,13},{10,... | collective-permute-start | bytes 159752 | tf_op jit(solution)/shard_map/ppermute | solution.py:382
  30.1 7.6 %collective-permute-start.12 = (bf16[64,128]{1,0:T(8,128)(2,1)S(1)}, bf16[64,128]{1,0:T(8,128)(2,1)S(1)}, u32[]{:S(2)}, u32[]{:S(2)}) collective-permute-start(bf16[64,128]{1,0:T(8,128)(2,1)S(1)} %get-tuple-element.41), channel_id=1, source_target_pairs={{0,1},{1,0},{2,3},{3,2},{4,5},{5,4},{6,7},{7,6},{8,9},{9,8},{10,11... | collective-permute-start | bytes 49160 | tf_op jit(solution)/shard_map/ppermute | solution.py:382
  30.2 7.5 %collective-permute-start.13 = (bf16[64,128]{1,0:T(8,128)(2,1)S(1)}, bf16[64,128]{1,0:T(8,128)(2,1)S(1)}, u32[]{:S(2)}, u32[]{:S(2)}) collective-permute-start(bf16[64,128]{1,0:T(8,128)(2,1)S(1)} %get-tuple-element.42), channel_id=1, source_target_pairs={{0,2},{1,3},{2,0},{3,1},{4,6},{5,7},{6,4},{7,5},{8,10},{9,11},{10,... | collective-permute-start | bytes 49160 | tf_op jit(solution)/shard_map/ppermute | solution.py:382
  31.7 6.0 %collective-permute-start.14 = (bf16[64,128]{1,0:T(8,128)(2,1)S(1)}, bf16[64,128]{1,0:T(8,128)(2,1)S(1)}, u32[]{:S(2)}, u32[]{:S(2)}) collective-permute-start(bf16[64,128]{1,0:T(8,128)(2,1)S(1)} %get-tuple-element.43), channel_id=1, source_target_pairs={{0,3},{1,2},{2,1},{3,0},{4,7},{5,6},{6,5},{7,4},{8,11},{9,10},{10,... | collective-permute-start | bytes 49160 | tf_op jit(solution)/shard_map/ppermute | solution.py:382

commit v3 on v2

--- a/solution.py
+++ b/solution.py
@@ -10,6 +10,7 @@
 
 HD = 128
 BLOCK = 128
+
 SLAB = 4
 F32 = jnp.float32
 BF16 = jnp.bfloat16
@@ -34,16 +35,20 @@
 
 def pack_stats(pairs):
     rows = []
-    for maximum, total in pairs:
-        rows += split3(maximum) + split3(total) + [jnp.zeros((2, HD), F32)]
+    for shift, total in pairs:
+        rows += [shift] + split3(total)
+    rows += [jnp.zeros((1, HD), F32)] * (stat_rows(len(pairs)) - len(rows))
     return jnp.concatenate(rows, axis=0)
 
 
+def stat_rows(kvq):
+    return -(-4 * kvq // 8) * 8
+
+
 def unpack_stats(stats, k):
-    at = 8 * k
-    maximum = stats[at : at + 1] + stats[at + 1 : at + 2] + stats[at + 2 : at + 3]
-    total = stats[at + 3 : at + 4] + stats[at + 4 : at + 5] + stats[at + 5 : at + 6]
-    return maximum, total
+    at = 4 * k
+    total = stats[at + 1 : at + 2] + stats[at + 2 : at + 3] + stats[at + 3 : at + 4]
+    return stats[at : at + 1], total
 
 
 def to_lanes(column):
@@ -61,7 +66,7 @@
     return jnp.sum(jnp.where(same, jnp.broadcast_to(lanes, (rows, HD)), 0.0), axis=1, keepdims=True)
 
 
-def prepare(me, queries, prompt_of, prompt_cache, kvq, group):
+def prepare(queries, prompt_of, blocks, prompt_cache, kvq, group):
     cands, width = queries.shape
     heads = width // HD
     prompts, span, kv_width2 = prompt_cache.shape
@@ -70,16 +75,23 @@
     part_rows = kvq * cands * group + 8
     kvw = kvq * HD
 
-    def kernel(me_ref, q_ref, ids_ref, cache_ref, all_ref, *rest):
+    def kernel(q_ref, ids_ref, blocks_ref, cache_ref, all_ref, live_ref, *rest):
         q_out = rest[:SLAB]
         kv_out = rest[SLAB : 2 * SLAB]
-        (scratch,) = rest[2 * SLAB :]
-        mine = me_ref[0]
+        scratch, held, sem = rest[2 * SLAB :]
+        mine = lax.axis_index("seq") % SLAB
+        fetches = []
+        for p in range(prompts):
+            fetch = pltpu.make_async_copy(cache_ref.at[p], held.at[p], sem.at[p])
+            fetch.start()
+            fetches.append(fetch)
         for h in range(heads):
             scratch[pl.ds(h, cands, stride=heads), :] = q_ref[:, h * HD : (h + 1) * HD].astype(F32)
         all_ref[...] = scratch[...].astype(BF16)
         id_rows = [jnp.full((1, HD), ids_ref[r].astype(F32)) for r in range(cands)]
         id_rows = id_rows + [jnp.zeros((8 - cands, HD), F32)]
+        for r in range(cands):
+            live_ref[r : r + 1, :] = jnp.full((1, HD), BLOCK * blocks_ref[r])
         for j in range(SLAB):
             first = (mine ^ j) * hq
             pieces = []
@@ -88,91 +100,94 @@
                     at = pl.multiple_of(r * heads + first + k * group, 8)
                     pieces.append(scratch[pl.ds(at, group), :])
             q_out[j][...] = jnp.concatenate(pieces + id_rows, axis=0).astype(BF16)
-        for j in range(SLAB):
-            for side in range(2):
-                column = pl.multiple_of(side * kv_width + (mine ^ j) * kvw, kvw)
-                kv_out[j][side] = cache_ref[:, :, pl.ds(column, kvw)]
+        for p in range(prompts):
+            fetches[p].wait()
+            for j in range(SLAB):
+                for side in range(2):
+                    column = pl.multiple_of(side * kv_width + (mine ^ j) * kvw, kvw)
+                    kv_out[j][side, p] = held[p, :, pl.ds(column, kvw)]
 
     smem = pl.BlockSpec(memory_space=pltpu.SMEM)
     out = pl.pallas_call(
         kernel,
-        out_shape=[pltpu.VMEM((cands * heads, HD), BF16)]
+        out_shape=[pltpu.VMEM((cands * heads, HD), BF16), pltpu.VMEM((8, HD), jnp.int32)]
         + [pltpu.VMEM((part_rows, HD), BF16)] * SLAB
         + [pltpu.VMEM((2, prompts, span, kvw), BF16)] * SLAB,
-        in_specs=[smem, vmem_spec(), smem, vmem_spec()],
-        out_specs=[vmem_spec()] * (1 + 2 * SLAB),
+        in_specs=[vmem_spec(), smem, smem, pl.BlockSpec(memory_space=pl.ANY)],
+        out_specs=[vmem_spec()] * (2 + 2 * SLAB),
         scratch_shapes=[
             pltpu.VMEM((cands * heads, HD), F32),
+            pltpu.VMEM((prompts, span, kv_width2), BF16),
+            pltpu.SemaphoreType.DMA((prompts,)),
         ],
         name="prepare",
-    )(me, queries, prompt_of, prompt_cache)
-    return out[0], out[1 : 1 + SLAB], out[1 + SLAB :]
-
-
-def suffix_attend(which, blocks, rows_q, suffix_cache, kv_heads):
+    )(queries, prompt_of, blocks, prompt_cache)
+    return out[0], out[1], out[2 : 2 + SLAB], out[2 + SLAB :]
+
+
+def suffix_attend(live, rows_q, suffix_cache, kv_heads):
     cands, length, kv_width2 = suffix_cache.shape
     kv_width = kv_width2 // 2
     heads = rows_q.shape[0] // cands
     group = heads // kv_heads
 
-    def kernel(blocks_ref, q_ref, cache_ref, max_ref, sum_ref, mix_ref, keys, values, sem):
-        fetches = [
-            pltpu.make_async_copy(
-                cache_ref.at[which, :, side * kv_width : (side + 1) * kv_width], target, sem.at[side]
-            )
-            for side, target in enumerate((keys, values))
-        ]
-        for fetch in fetches:
-            fetch.start()
-        q = q_ref[which * heads : (which + 1) * heads, :]
-        wide = jnp.concatenate([q] * kv_heads, axis=1)
+    def kernel(live_ref, q_ref, cache_ref, max_ref, sum_ref, mix_ref, keys, values, sem):
+        fetches = []
+        for c in range(cands):
+            for side, target in enumerate((keys, values)):
+                fetch = pltpu.make_async_copy(
+                    cache_ref.at[c, :, side * kv_width : (side + 1) * kv_width],
+                    target.at[c],
+                    sem.at[c, side],
+                )
+                fetch.start()
+                fetches.append(fetch)
         diagonal = (
             lax.broadcasted_iota(jnp.int32, (heads, kv_width), 0) // group
             == lax.broadcasted_iota(jnp.int32, (heads, kv_width), 1) // HD
         )
-        wide = jnp.where(diagonal, wide, jnp.zeros_like(wide))
-        fetches[0].wait()
-        logits = lax.dot_general(
-            wide,
-            keys[...],
-            (((1,), (1,)), ((), ())),
-            preferred_element_type=F32,
-        ) * HD ** (-0.5)
-        live = lax.broadcasted_iota(jnp.int32, (heads, length), 1) < BLOCK * blocks_ref[which]
-        logits = jnp.where(live, logits, floor_logit)
-        maxima = jnp.max(logits, axis=1, keepdims=True)
-        exponent = jnp.where(live, jnp.exp(logits - maxima), 0.0)
-        totals = jnp.sum(exponent, axis=1, keepdims=True)
-        fetches[1].wait()
-        mixed = jnp.dot(exponent.astype(BF16), values[...], preferred_element_type=F32)
-        max_ref[...] = jnp.broadcast_to(maxima, (heads, HD))
-        sum_ref[...] = jnp.broadcast_to(totals, (heads, HD))
-        for k in range(kv_heads):
-            mix_ref[k * group : (k + 1) * group, :] = mixed[
-                k * group : (k + 1) * group, k * HD : (k + 1) * HD
-            ]
+        position = lax.broadcasted_iota(jnp.int32, (heads, length), 1)
+        for c in range(cands):
+            rows = slice(c * heads, (c + 1) * heads)
+            wide = jnp.concatenate([q_ref[rows, :]] * kv_heads, axis=1)
+            wide = jnp.where(diagonal, wide, jnp.zeros_like(wide))
+            fetches[2 * c].wait()
+            logits = lax.dot_general(
+                wide, keys[c], (((1,), (1,)), ((), ())), preferred_element_type=F32
+            ) * HD ** (-0.5)
+            live_row = jnp.concatenate([live_ref[c : c + 1, :]] * (length // HD), axis=1)
+            live = position < live_row
+            logits = jnp.where(live, logits, floor_logit)
+            maxima = jnp.max(logits, axis=1, keepdims=True)
+            exponent = jnp.where(live, jnp.exp(logits - maxima), 0.0)
+            totals = jnp.sum(exponent, axis=1, keepdims=True)
+            fetches[2 * c + 1].wait()
+            mixed = jnp.dot(exponent.astype(BF16), values[c], preferred_element_type=F32)
+            max_ref[rows, :] = jnp.broadcast_to(maxima, (heads, HD))
+            sum_ref[rows, :] = jnp.broadcast_to(totals, (heads, HD))
+            for k in range(kv_heads):
+                at = c * heads + k * group
+                mix_ref[at : at + group, :] = mixed[
+                    k * group : (k + 1) * group, k * HD : (k + 1) * HD
+                ]
 
     return pl.pallas_call(
         kernel,
-        out_shape=[pltpu.VMEM((heads, HD), F32)] * 3,
-        in_specs=[
-            pl.BlockSpec(memory_space=pltpu.SMEM),
-            vmem_spec(),
-            pl.BlockSpec(memory_space=pl.ANY),
-        ],
+        out_shape=[pltpu.VMEM((cands * heads, HD), F32)] * 3,
+        in_specs=[vmem_spec(), vmem_spec(), pl.BlockSpec(memory_space=pl.ANY)],
         out_specs=[vmem_spec()] * 3,
         scratch_shapes=[
-            pltpu.VMEM((length, kv_width), BF16),
-            pltpu.VMEM((length, kv_width), BF16),
-            pltpu.SemaphoreType.DMA((2,)),
+            pltpu.VMEM((cands, length, kv_width), BF16),
+            pltpu.VMEM((cands, length, kv_width), BF16),
+            pltpu.SemaphoreType.DMA((cands, 2)),
         ],
         cost_estimate=pl.CostEstimate(
-            flops=4 * heads * length * kv_width,
-            transcendentals=heads * length,
-            bytes_accessed=2 * suffix_cache.size // cands,
+            flops=4 * cands * heads * length * kv_width,
+            transcendentals=cands * heads * length,
+            bytes_accessed=2 * suffix_cache.size,
         ),
         name="suffix",
-    )(blocks, *near([rows_q]), suffix_cache)
+    )(*near([live, rows_q]), suffix_cache)
 
 
 def prompt_attend(query_blocks, caches, cands, kvq, group):
@@ -182,9 +197,8 @@
     part = cands * group
     part_rows = kvq * part + 8
     block_rows = SLAB * part
-    out_rows = kvq * block_rows + 8 * kvq
-    prompts, span = caches[0].shape[1:3]
-    width = SLAB * span
+    out_rows = kvq * block_rows + stat_rows(kvq)
+    prompts, _ = caches[0].shape[1:3]
 
     def kernel(*refs):
         if stacked:
@@ -203,7 +217,6 @@
                     at = j * part_rows + kvq * part + r
                     ids.append(jnp.broadcast_to(rows[i][at : at + 1], (group, HD)))
         ids = jnp.concatenate(ids, axis=0)
-        ids = jnp.concatenate([ids] * (width // HD), axis=1)
         picked = [ids == float(p) for p in range(prompts)]
         stats = [[] for _ in range(chunk)]
         for k in range(kvq):
@@ -214,28 +227,30 @@
                     for j in range(SLAB)
                 ],
                 axis=0,
-            ).astype(BF16)
-            logits = None
-            for p in range(prompts):
-                keys = jnp.concatenate(
-                    [ref[0, p, :, k * HD : (k + 1) * HD] for ref in cache_refs], axis=0
+            )
+            q = jnp.concatenate([jnp.where(one, q, 0.0) for one in picked], axis=1).astype(BF16)
+
+            def both(side):
+                return jnp.concatenate(
+                    [
+                        jnp.concatenate(
+                            [ref[side, p, :, k * HD : (k + 1) * HD] for p in range(prompts)], axis=1
+                        )
+                        for ref in cache_refs
+                    ],
+                    axis=0,
                 )
-                one = lax.dot_general(
-                    q, keys, (((1,), (1,)), ((), ())), preferred_element_type=F32
-                )
-                logits = one if logits is None else jnp.where(picked[p], one, logits)
-            logits = logits * HD ** (-0.5)
-            maxima = jnp.max(logits, axis=1, keepdims=True)
+
+            logits = lax.dot_general(
+                q, both(0), (((1,), (1,)), ((), ())), preferred_element_type=F32
+            ) * HD ** (-0.5)
+            maxima = jnp.max(logits, axis=1, keepdims=True).astype(BF16).astype(F32)
             exponent = jnp.exp(logits - maxima)
             totals = jnp.sum(exponent, axis=1, keepdims=True)
-            mixed = None
-            for p in range(prompts):
-                values = jnp.concatenate(
-                    [ref[1, p, :, k * HD : (k + 1) * HD] for ref in cache_refs], axis=0
-                )
-                weights = jnp.where(picked[p], exponent, 0.0).astype(BF16)
-                one = jnp.dot(weights, values, preferred_element_type=F32)
-                mixed = one if mixed is None else mixed + one
+            wide = jnp.dot(exponent.astype(BF16), both(1), preferred_element_type=F32)
+            mixed = wide[:, :HD]
+            for p in range(1, prompts):
+                mixed = jnp.where(picked[p], wide[:, p * HD : (p + 1) * HD], mixed)
             for i in range(chunk):
                 cut = slice(i * block_rows, (i + 1) * block_rows)
                 out_refs[i][k * block_rows : (k + 1) * block_rows, :] = mixed[cut].astype(BF16)
@@ -269,7 +284,7 @@
     outer = blocks.shape[0] if stacked else len(blocks)
     part = cands * group
     block_rows = SLAB * part
-    out_rows = kvq * part + 8 * kvq
+    out_rows = kvq * part + stat_rows(kvq)
 
     def kernel(*refs):
         if stacked:
@@ -312,16 +327,15 @@
     )(*near(args))
 
 
-def finish(me, pieces, suffix_state, reward, cands, kvq, group):
+def finish(pieces, suffix_state, reward, cands, kvq, group):
     part = cands * group
     hq = kvq * group
     heads = SLAB * hq
 
-    def kernel(me_ref, *refs):
+    def kernel(*refs):
         piece_refs = refs[:SLAB]
-        state_refs = refs[SLAB : SLAB + 3 * cands]
-        reward_ref, out_ref, score_ref, scratch = refs[SLAB + 3 * cands :]
-        mine = me_ref[0]
+        max_ref, sum_ref, mix_ref, reward_ref, out_ref, score_ref, scratch = refs[SLAB:]
+        mine = lax.axis_index("seq") % SLAB
         scores = [jnp.zeros((group, HD), F32) for _ in range(cands)]
         for j in range(SLAB):
             first = (mine ^ j) * hq
@@ -333,9 +347,7 @@
                 total = to_rows(total, part, j * part)
                 weight = reward_ref[pl.ds(pl.multiple_of(first + k * group, 8), group), :]
                 for r in range(cands):
-                    max_ref, sum_ref, mix_ref = state_refs[3 * r : 3 * r + 3]
-                    at = pl.ds(pl.multiple_of(first + k * group, 8), group)
-                    row = pl.ds(pl.multiple_of(r * heads + first + k * group, 8), group)
+                    at = pl.ds(pl.multiple_of(r * heads + first + k * group, 8), group)
                     cut = slice(r * group, (r + 1) * group)
                     home_max = max_ref[at, :]
                     here_max = jnp.broadcast_to(maximum[cut], (group, HD))
@@ -345,7 +357,7 @@
                     total_all = home * sum_ref[at, :] + here * total[cut]
                     mixed = home * mix_ref[at, :] + here * mix[k * part :][cut]
                     attended = (mixed / total_all).astype(BF16).astype(F32)
-                    scratch[row, :] = attended
+                    scratch[at, :] = attended
                     scores[r] = scores[r] + attended * weight
         for h in range(heads):
             out_ref[:, h * HD : (h + 1) * HD] = scratch[pl.ds(h, cands, stride=heads), :].astype(
@@ -361,11 +373,11 @@
             jax.ShapeDtypeStruct((cands, heads * HD), BF16),
             jax.ShapeDtypeStruct((cands,), F32),
         ],
-        in_specs=[smem] + [vmem_spec()] * (SLAB + 3 * cands + 1),
+        in_specs=[vmem_spec()] * (SLAB + 4),
         out_specs=[vmem_spec(), smem],
         scratch_shapes=[pltpu.VMEM((cands * heads, HD), F32)],
         name="finish",
-    )(me, *near(pieces), *near(suffix_state), reward)
+    )(*near(pieces), *near(suffix_state), *near([reward]))
 
 
 def attend(queries, prompt_of, suffix_cache, suffix_blocks, prompt_cache, reward_weight):
@@ -376,7 +388,6 @@
     kvq = kv_heads // SLAB
     devices = lax.axis_size("seq")
     outer = devices // SLAB
-    me = jnp.reshape(lax.axis_index("seq") % SLAB, (1,)).astype(jnp.int32)
 
     def hop(x, step):
         return lax.ppermute(x, "seq", [(i, i ^ step) for i in range(devices)])
@@ -387,13 +398,13 @@
     direct = is_direct(devices)
     columns = [[SLAB * z + i for z in range(outer)] for i in range(SLAB)]
 
-    rows_q, q_parts, kv_parts = prepare(me, queries, prompt_of[:, 0], prompt_cache, kvq, group)
+    rows_q, live, q_parts, kv_parts = prepare(
+        queries, prompt_of[:, 0], suffix_blocks, prompt_cache, kvq, group
+    )
     q_parts = spread(q_parts, 1)
     kv_parts = spread(kv_parts, 1)
     q_slab = jnp.concatenate(q_parts, axis=0)
-    suffix_state = []
-    for c in range(cands):
-        suffix_state += suffix_attend(c, suffix_blocks, rows_q, suffix_cache, kv_heads)
+    suffix_state = suffix_attend(live, rows_q, suffix_cache, kv_heads)
     if direct:
         q_all = spread([q_slab] * outer, SLAB)
     else:
@@ -407,7 +418,7 @@
         )
     pieces = spread(merge(partial, cands, kvq, group), 1)
     reward = reward_weight.reshape(heads, HD)
-    return tuple(finish(me, pieces, suffix_state, reward, cands, kvq, group))
+    return tuple(finish(pieces, suffix_state, reward, cands, kvq, group))
 
 
 def is_direct(devices):

time: 39.7 us -> 38.4 us (0.967)
  waiting for transfers between devices: 5.54 us -> 12.3 us
  Pallas kernels: 13.3 us -> 8.24 us
  starting transfers between devices: 19.7 us -> 16.8 us
    ppermute x15, waiting for transfers between devices: 5.54 us -> 12.3 us  [hop(): return lax.ppermute(x, 'seq', [(i, i ^ step) for i in range(devices)])]
    pallas_call x4 -> x2, Pallas kernels: 9.93 us -> 6.17 us  [the longest x1 4.02 us: suffix_attend(): pl.pallas_call(kernel, out_shape=[pltpu.VMEM((cands * heads, HD), F32)] *...]
    ppermute x15, starting transfers between devices: 19.7 us -> 16.8 us  [hop(): return lax.ppermute(x, 'seq', [(i, i ^ step) for i in range(devices)])]
    pallas_call x1, Pallas kernels: 1.64 us -> 0.87 us  [finish(): pl.pallas_call(kernel, out_shape=[jax.ShapeDtypeStruct((cands, heads * HD...]
    pallas_call x1, Pallas kernels: 1.53 us -> 1.01 us  [prompt_attend(): pl.pallas_call(kernel, out_shape=[pltpu.VMEM((out_rows, HD), BF16)] * out...]
  transfers between devices with their start and end apart: 15 -> 15, of which waited for: 5 -> 7; matrix products, arithmetic and copies ran while one was open for 0% -> 0% of each run, Pallas kernels for 21% -> 11%
where the time goes in v3:
time: 38.4 us; the launch traced here: 38.2 us
  starting transfers between devices  16.8 us (44%)
  waiting for transfers between devices  12.3 us (32%)
  Pallas kernels  8.24 us (21%)
  between operations  0.74 us (2%)
    ppermute x15, starting transfers between devices, hop(): return lax.ppermute(x, 'seq', [(i, i ^ step) for i in range(devices)])  16.8 us
    ppermute x15, waiting for transfers between devices, hop(): return lax.ppermute(x, 'seq', [(i, i ^ step) for i in range(devices)])  12.3 us
    pallas_call x1, Pallas kernels, suffix_attend(): pl.pallas_call(kernel, out_shape=[pltpu.VMEM((cands * heads, HD), F32)] *...  4.02 us
    pallas_call x1, Pallas kernels, prepare(): pl.pallas_call(kernel, out_shape=[pltpu.VMEM((cands * heads, HD), BF16),...  2.15 us
    pallas_call x1, Pallas kernels, prompt_attend(): pl.pallas_call(kernel, out_shape=[pltpu.VMEM((out_rows, HD), BF16)] * out...  1.01 us
    pallas_call x1, Pallas kernels, finish(): pl.pallas_call(kernel, out_shape=[jax.ShapeDtypeStruct((cands, heads * HD...  0.87 us
  transfers between devices with their start and end apart: 15, of which 7 were waited for; matrix products, arithmetic and copies ran while one was open for 0% of the time, Pallas kernels for 11%

profile of v3, /device:TPU:0, one launch (start us, length us, event | category | flops | bytes accessed | tf_op | source)
XLA Modules:
  0.0 38.2 jit_solution(4530607895798680915)
XLA Ops:
  0.6 0.0 copy-start
  0.6 2.1 %prepare.1 = (bf16[192,128]{1,0:T(8,128)(2,1)S(1)}, s32[8,128]{1,0:T(8,128)S(1)}, bf16[56,128]{1,0:T(8,128)(2,1)S(1)}, bf16[56,128]{1,0:T(8,128)(2,1)S(1)}, bf16...) custom-call(bf16[3,8192]{1,0:T(4,128)(2,1)} %q_ref.1, ...), custom_call_target="tpu_custom_call" | custom-call | tf_op jit(solution)/shard_map/prepare/pallas_call | solution.py:111
  2.8 0.6 %collective-permute-start = (bf16[56,128]{1,0:T(8,128)(2,1)S(1)}, bf16[56,128]{1,0:T(8,128)(2,1)S(1)}, u32[]{:S(2)}, u32[]{:S(2)}) collective-permute-start(bf16[56,128]{1,0:T(8,128)(2,1)S(1)} %get-tuple-element.24), channel_id=1, source_target_pairs={{0,1},{1,0},{2,3},{3,2},{4,5},{5,4},{6,7},{7,6},{8,9},{9,8},{10,11... | collective-permute-start | bytes 43016 | tf_op jit(solution)/shard_map/ppermute | solution.py:393
  3.4 2.6 %collective-permute-start.1 = (bf16[56,128]{1,0:T(8,128)(2,1)S(1)}, bf16[56,128]{1,0:T(8,128)(2,1)S(1)}, u32[]{:S(2)}, u32[]{:S(2)}) collective-permute-start(bf16[56,128]{1,0:T(8,128)(2,1)S(1)} %get-tuple-element.25), channel_id=1, source_target_pairs={{0,2},{1,3},{2,0},{3,1},{4,6},{5,7},{6,4},{7,5},{8,10},{9,11},{10,... | collective-permute-start | bytes 43016 | tf_op jit(solution)/shard_map/ppermute | solution.py:393
  5.9 0.0 collective-permute-start.2
  6.0 0.2 collective-permute-start.6
  6.1 1.9 %collective-permute-start.7 = (bf16[2,2,128,256]{3,2,1,0:T(8,128)(2,1)S(1)}, bf16[2,2,128,256]{3,2,1,0:T(8,128)(2,1)S(1)}, u32[]{:S(2)}, u32[]{:S(2)}) collective-permute-start(bf16[2,2,128,256]{3,2,1,0:T(8,128)(2,1)S(1)} %get-tuple-element.29), channel_id=1, source_target_pairs={{0,2},{1,3},{2,0},{3,1},{4,6},{5,7},{6,4},{7,5},{8,10},{9,11},{10,... | collective-permute-start | bytes 786440 | tf_op jit(solution)/shard_map/ppermute | solution.py:393
  8.1 0.0 collective-permute-done
  8.1 0.0 collective-permute-start.8
  8.1 0.0 collective-permute-done.1
  8.1 1.0 %collective-permute-done.2 = bf16[56,128]{1,0:T(8,128)(2,1)S(1)} collective-permute-done((bf16[56,128]{1,0:T(8,128)(2,1)S(1)}, bf16[56,128]{1,0:T(8,128)(2,1)S(1)}, u32[]{:S(2)}, u32[]{:S(2)}) %collective-permute-start.2) | collective-permute-done | bytes 14368 | tf_op jit(solution)/shard_map/ppermute | solution.py:393
  9.1 3.6 %collective-permute-start.5 = (bf16[224,128]{1,0:T(8,128)(2,1)S(1)}, bf16[224,128]{1,0:T(8,128)(2,1)S(1)}, u32[]{:S(2)}, u32[]{:S(2)}) collective-permute-start(bf16[224,128]{1,0:T(8,128)(2,1)S(1)} %constant_dynamic-update-slice_fusion.refs_0_), channel_id=1, source_target_pairs={{0,12},{1,13},{2,14},{3,15},{4,8},{5,9},{6,10},{7,11},{8,4},{9,5},... | collective-permute-start | bytes 172040 | tf_op jit(solution)/shard_map/ppermute | solution.py:393
  12.7 0.0 collective-permute-start.4
  12.7 2.4 %collective-permute-done.5.refs_3_ = bf16[224,128]{1,0:T(8,128)(2,1)S(1)} collective-permute-done((bf16[224,128]{1,0:T(8,128)(2,1)S(1)}, bf16[224,128]{1,0:T(8,128)(2,1)S(1)}, u32[]{:S(2)}, u32[]{:S(2)}) %collective-permute-start.5) | collective-permute-done | bytes 57376 | tf_op jit(solution)/shard_map/ppermute | solution.py:393
  15.1 1.6 %collective-permute-start.3 = (bf16[224,128]{1,0:T(8,128)(2,1)S(1)}, bf16[224,128]{1,0:T(8,128)(2,1)S(1)}, u32[]{:S(2)}, u32[]{:S(2)}) collective-permute-start(bf16[224,128]{1,0:T(8,128)(2,1)S(1)} %constant_dynamic-update-slice_fusion.refs_0_), channel_id=1, source_target_pairs={{0,4},{1,5},{2,6},{3,7},{4,0},{5,1},{6,2},{7,3},{8,12},{9,13},{10,... | collective-permute-start | bytes 172040 | tf_op jit(solution)/shard_map/ppermute | solution.py:393
  16.7 1.4 %collective-permute-done.4.refs_2_ = bf16[224,128]{1,0:T(8,128)(2,1)S(1)} collective-permute-done((bf16[224,128]{1,0:T(8,128)(2,1)S(1)}, bf16[224,128]{1,0:T(8,128)(2,1)S(1)}, u32[]{:S(2)}, u32[]{:S(2)}) %collective-permute-start.4) | collective-permute-done | bytes 57376 | tf_op jit(solution)/shard_map/ppermute | solution.py:393
  18.1 1.2 %collective-permute-done.3.refs_1_ = bf16[224,128]{1,0:T(8,128)(2,1)S(1)} collective-permute-done((bf16[224,128]{1,0:T(8,128)(2,1)S(1)}, bf16[224,128]{1,0:T(8,128)(2,1)S(1)}, u32[]{:S(2)}, u32[]{:S(2)}) %collective-permute-start.3) | collective-permute-done | bytes 57376 | tf_op jit(solution)/shard_map/ppermute | solution.py:393
  19.3 0.0 collective-permute-done.6.refs_5_
  19.3 0.0 collective-permute-done.7.refs_6_
  19.3 0.7 %collective-permute-done.8.refs_7_ = bf16[2,2,128,256]{3,2,1,0:T(8,128)(2,1)S(1)} collective-permute-done((bf16[2,2,128,256]{3,2,1,0:T(8,128)(2,1)S(1)}, bf16[2,2,128,256]{3,2,1,0:T(8,128)(2,1)S(1)}, u32[]{:S(2)}, u32[]{:S(2)}) %collective-permute-start.8) | collective-permute-done | bytes 262176 | tf_op jit(solution)/shard_map/ppermute | solution.py:393
  20.0 1.0 %prompt.1 = (bf16[200,128]{1,0:T(8,128)(2,1)S(1)}, bf16[200,128]{1,0:T(8,128)(2,1)S(1)}, bf16[200,128]{1,0:T(8,128)(2,1)S(1)}, bf16[200,128]{1,0:T(8,128)(2,1)S(1)}) custom-call(bf16[224,128]{1,0:T(8,128)(2,1)S(1)} %constant_dynamic-update-slice_fusion.refs_0_, bf16[224,128]{1,0:T(8,128)(2,1)S(1)} %collective-permute-done.3.refs_1_, ...), custom_call_target="tpu_custom_call" | custom-call | tf_op jit(solution)/shard_map/prompt/pallas_call | solution.py:273
  21.0 1.6 %collective-permute-start.9 = (bf16[200,128]{1,0:T(8,128)(2,1)S(1)}, bf16[200,128]{1,0:T(8,128)(2,1)S(1)}, u32[]{:S(2)}, u32[]{:S(2)}) collective-permute-start(bf16[200,128]{1,0:T(8,128)(2,1)S(1)} %get-tuple-element.32), channel_id=1, source_target_pairs={{0,4},{1,5},{2,6},{3,7},{4,0},{5,1},{6,2},{7,3},{8,12},{9,13},{10,... | collective-permute-start | bytes 153608 | tf_op jit(solution)/shard_map/ppermute | solution.py:393
  22.6 2.6 %collective-permute-start.10 = (bf16[200,128]{1,0:T(8,128)(2,1)S(1)}, bf16[200,128]{1,0:T(8,128)(2,1)S(1)}, u32[]{:S(2)}, u32[]{:S(2)}) collective-permute-start(bf16[200,128]{1,0:T(8,128)(2,1)S(1)} %get-tuple-element.33), channel_id=1, source_target_pairs={{0,8},{1,9},{2,10},{3,11},{4,12},{5,13},{6,14},{7,15},{8,0},{9,1},... | collective-permute-start | bytes 153608 | tf_op jit(solution)/shard_map/ppermute | solution.py:393
  25.2 0.3 collective-permute-start.11
  25.5 0.0 collective-permute-done.9.refs_1_
  25.5 3.4 %collective-permute-done.10.refs_2_ = bf16[200,128]{1,0:T(8,128)(2,1)S(1)} collective-permute-done((bf16[200,128]{1,0:T(8,128)(2,1)S(1)}, bf16[200,128]{1,0:T(8,128)(2,1)S(1)}, u32[]{:S(2)}, u32[]{:S(2)}) %collective-permute-start.10) | collective-permute-done | bytes 51232 | tf_op jit(solution)/shard_map/ppermute | solution.py:393
  28.8 2.2 %collective-permute-done.11.refs_3_ = bf16[200,128]{1,0:T(8,128)(2,1)S(1)} collective-permute-done((bf16[200,128]{1,0:T(8,128)(2,1)S(1)}, bf16[200,128]{1,0:T(8,128)(2,1)S(1)}, u32[]{:S(2)}, u32[]{:S(2)}) %collective-permute-start.11) | collective-permute-done | bytes 51232 | tf_op jit(solution)/shard_map/ppermute | solution.py:393
  31.1 0.2 merge.1
  31.3 0.1 collective-permute-start.12
  31.4 1.4 %collective-permute-start.13 = (bf16[56,128]{1,0:T(8,128)(2,1)S(1)}, bf16[56,128]{1,0:T(8,128)(2,1)S(1)}, u32[]{:S(2)}, u32[]{:S(2)}) collective-permute-start(bf16[56,128]{1,0:T(8,128)(2,1)S(1)} %get-tuple-element.37), channel_id=1, source_target_pairs={{0,2},{1,3},{2,0},{3,1},{4,6},{5,7},{6,4},{7,5},{8,10},{9,11},{10,... | collective-permute-start | bytes 43016 | tf_op jit(solution)/shard_map/ppermute | solution.py:393
  32.7 0.5 %collective-permute-start.14 = (bf16[56,128]{1,0:T(8,128)(2,1)S(1)}, bf16[56,128]{1,0:T(8,128)(2,1)S(1)}, u32[]{:S(2)}, u32[]{:S(2)}) collective-permute-start(bf16[56,128]{1,0:T(8,128)(2,1)S(1)} %get-tuple-element.38), channel_id=1, source_target_pairs={{0,3},{1,2},{2,1},{3,0},{4,7},{5,6},{6,5},{7,4},{8,11},{9,10},{10,... | collective-permute-start | bytes 43016 | tf_op jit(solution)/shard_map/ppermute | solution.py:393
  33.2 4.0 %suffix.1 = (f32[192,128]{1,0:T(8,128)S(1)}, f32[192,128]{1,0:T(8,128)S(1)}, f32[192,128]{1,0:T(8,128)S(1)}) custom-call(s32[8,128]{1,0:T(8,128)S(1)} %get-tuple-element.39.live_ref, bf16[192,128]{1,0:T(8,128)(2,1)S(1)} %get-tuple-element.40.q_ref, bf16[3,512,2048]{2,1,0:T(8,128)(2,1)} %cache_ref.3), custom_call_target="tpu_custom_call" | custom-call | flops 402653184 | bytes 6291456 | tf_op jit(solution)/shard_map/suffix/pallas_call | solution.py:174
  37.2 0.0 collective-permute-done.12.refs_1_
  37.3 0.0 collective-permute-done.13.refs_2_
  37.3 0.0 collective-permute-done.14.refs_3_
  37.3 0.0 copy-done
  37.3 0.9 %finish.1 = (bf16[3,8192]{1,0:T(4,128)(2,1)}, f32[3]{0:T(128)}) custom-call(bf16[56,128]{1,0:T(8,128)(2,1)S(1)} %get-tuple-element.35.refs_0_, bf16[56,128]{1,0:T(8,128)(2,1)S(1)} %collective-permute-done.12.refs_1_, bf16[56,128]{1,0:T(8,128)(2,1)S(1)} %collective-permute-done.13.refs_2_, bf16[56,128]{1,0:T(8,128)(2,1)S(1)} %collective-permute-done.14.refs_3_, ...), custom_call_target="tpu_custom_call" | custom-call | tf_op jit(solution)/shard_map/finish/pallas_call | solution.py:370
  (4 shorter events, 0.0 us)
Async XLA Ops:
  0.6 36.7 %copy-start = (f32[8192]{0:T(1024)S(1)}, f32[8192]{0:T(1024)}, u32[]{:S(2)}) copy-start(f32[8192]{0:T(1024)} %param.11) | copy-start | bytes 98308
  2.8 5.3 %collective-permute-start = (bf16[56,128]{1,0:T(8,128)(2,1)S(1)}, bf16[56,128]{1,0:T(8,128)(2,1)S(1)}, u32[]{:S(2)}, u32[]{:S(2)}) collective-permute-start(bf16[56,128]{1,0:T(8,128)(2,1)S(1)} %get-tuple-element.24), channel_id=1, source_target_pairs={{0,1},{1,0},{2,3},{3,2},{4,5},{5,4},{6,7},{7,6},{8,9},{9,8},{10,11... | collective-permute-start | bytes 43016 | tf_op jit(solution)/shard_map/ppermute | solution.py:393
  3.4 4.8 %collective-permute-start.1 = (bf16[56,128]{1,0:T(8,128)(2,1)S(1)}, bf16[56,128]{1,0:T(8,128)(2,1)S(1)}, u32[]{:S(2)}, u32[]{:S(2)}) collective-permute-start(bf16[56,128]{1,0:T(8,128)(2,1)S(1)} %get-tuple-element.25), channel_id=1, source_target_pairs={{0,2},{1,3},{2,0},{3,1},{4,6},{5,7},{6,4},{7,5},{8,10},{9,11},{10,... | collective-permute-start | bytes 43016 | tf_op jit(solution)/shard_map/ppermute | solution.py:393
  5.9 3.1 %collective-permute-start.2 = (bf16[56,128]{1,0:T(8,128)(2,1)S(1)}, bf16[56,128]{1,0:T(8,128)(2,1)S(1)}, u32[]{:S(2)}, u32[]{:S(2)}) collective-permute-start(bf16[56,128]{1,0:T(8,128)(2,1)S(1)} %get-tuple-element.26), channel_id=1, source_target_pairs={{0,3},{1,2},{2,1},{3,0},{4,7},{5,6},{6,5},{7,4},{8,11},{9,10},{10,... | collective-permute-start | bytes 43016 | tf_op jit(solution)/shard_map/ppermute | solution.py:393
  6.0 13.3 %collective-permute-start.6 = (bf16[2,2,128,256]{3,2,1,0:T(8,128)(2,1)S(1)}, bf16[2,2,128,256]{3,2,1,0:T(8,128)(2,1)S(1)}, u32[]{:S(2)}, u32[]{:S(2)}) collective-permute-start(bf16[2,2,128,256]{3,2,1,0:T(8,128)(2,1)S(1)} %get-tuple-element.28), channel_id=1, source_target_pairs={{0,1},{1,0},{2,3},{3,2},{4,5},{5,4},{6,7},{7,6},{8,9},{9,8},{10,11... | collective-permute-start | bytes 786440 | tf_op jit(solution)/shard_map/ppermute | solution.py:393
  6.1 13.2 %collective-permute-start.7 = (bf16[2,2,128,256]{3,2,1,0:T(8,128)(2,1)S(1)}, bf16[2,2,128,256]{3,2,1,0:T(8,128)(2,1)S(1)}, u32[]{:S(2)}, u32[]{:S(2)}) collective-permute-start(bf16[2,2,128,256]{3,2,1,0:T(8,128)(2,1)S(1)} %get-tuple-element.29), channel_id=1, source_target_pairs={{0,2},{1,3},{2,0},{3,1},{4,6},{5,7},{6,4},{7,5},{8,10},{9,11},{10,... | collective-permute-start | bytes 786440 | tf_op jit(solution)/shard_map/ppermute | solution.py:393
  8.1 11.9 %collective-permute-start.8 = (bf16[2,2,128,256]{3,2,1,0:T(8,128)(2,1)S(1)}, bf16[2,2,128,256]{3,2,1,0:T(8,128)(2,1)S(1)}, u32[]{:S(2)}, u32[]{:S(2)}) collective-permute-start(bf16[2,2,128,256]{3,2,1,0:T(8,128)(2,1)S(1)} %get-tuple-element.30), channel_id=1, source_target_pairs={{0,3},{1,2},{2,1},{3,0},{4,7},{5,6},{6,5},{7,4},{8,11},{9,10},{10,... | collective-permute-start | bytes 786440 | tf_op jit(solution)/shard_map/ppermute | solution.py:393
  9.1 6.0 %collective-permute-start.5 = (bf16[224,128]{1,0:T(8,128)(2,1)S(1)}, bf16[224,128]{1,0:T(8,128)(2,1)S(1)}, u32[]{:S(2)}, u32[]{:S(2)}) collective-permute-start(bf16[224,128]{1,0:T(8,128)(2,1)S(1)} %constant_dynamic-update-slice_fusion.refs_0_), channel_id=1, source_target_pairs={{0,12},{1,13},{2,14},{3,15},{4,8},{5,9},{6,10},{7,11},{8,4},{9,5},... | collective-permute-start | bytes 172040 | tf_op jit(solution)/shard_map/ppermute | solution.py:393
  12.7 5.4 %collective-permute-start.4 = (bf16[224,128]{1,0:T(8,128)(2,1)S(1)}, bf16[224,128]{1,0:T(8,128)(2,1)S(1)}, u32[]{:S(2)}, u32[]{:S(2)}) collective-permute-start(bf16[224,128]{1,0:T(8,128)(2,1)S(1)} %constant_dynamic-update-slice_fusion.refs_0_), channel_id=1, source_target_pairs={{0,8},{1,9},{2,10},{3,11},{4,12},{5,13},{6,14},{7,15},{8,0},{9,1},... | collective-permute-start | bytes 172040 | tf_op jit(solution)/shard_map/ppermute | solution.py:393
  15.1 4.2 %collective-permute-start.3 = (bf16[224,128]{1,0:T(8,128)(2,1)S(1)}, bf16[224,128]{1,0:T(8,128)(2,1)S(1)}, u32[]{:S(2)}, u32[]{:S(2)}) collective-permute-start(bf16[224,128]{1,0:T(8,128)(2,1)S(1)} %constant_dynamic-update-slice_fusion.refs_0_), channel_id=1, source_target_pairs={{0,4},{1,5},{2,6},{3,7},{4,0},{5,1},{6,2},{7,3},{8,12},{9,13},{10,... | collective-permute-start | bytes 172040 | tf_op jit(solution)/shard_map/ppermute | solution.py:393
  21.0 4.5 %collective-permute-start.9 = (bf16[200,128]{1,0:T(8,128)(2,1)S(1)}, bf16[200,128]{1,0:T(8,128)(2,1)S(1)}, u32[]{:S(2)}, u32[]{:S(2)}) collective-permute-start(bf16[200,128]{1,0:T(8,128)(2,1)S(1)} %get-tuple-element.32), channel_id=1, source_target_pairs={{0,4},{1,5},{2,6},{3,7},{4,0},{5,1},{6,2},{7,3},{8,12},{9,13},{10,... | collective-permute-start | bytes 153608 | tf_op jit(solution)/shard_map/ppermute | solution.py:393
  22.6 6.3 %collective-permute-start.10 = (bf16[200,128]{1,0:T(8,128)(2,1)S(1)}, bf16[200,128]{1,0:T(8,128)(2,1)S(1)}, u32[]{:S(2)}, u32[]{:S(2)}) collective-permute-start(bf16[200,128]{1,0:T(8,128)(2,1)S(1)} %get-tuple-element.33), channel_id=1, source_target_pairs={{0,8},{1,9},{2,10},{3,11},{4,12},{5,13},{6,14},{7,15},{8,0},{9,1},... | collective-permute-start | bytes 153608 | tf_op jit(solution)/shard_map/ppermute | solution.py:393
  25.2 5.9 %collective-permute-start.11 = (bf16[200,128]{1,0:T(8,128)(2,1)S(1)}, bf16[200,128]{1,0:T(8,128)(2,1)S(1)}, u32[]{:S(2)}, u32[]{:S(2)}) collective-permute-start(bf16[200,128]{1,0:T(8,128)(2,1)S(1)} %get-tuple-element.34), channel_id=1, source_target_pairs={{0,12},{1,13},{2,14},{3,15},{4,8},{5,9},{6,10},{7,11},{8,4},{9,5},... | collective-permute-start | bytes 153608 | tf_op jit(solution)/shard_map/ppermute | solution.py:393
  31.3 6.0 %collective-permute-start.12 = (bf16[56,128]{1,0:T(8,128)(2,1)S(1)}, bf16[56,128]{1,0:T(8,128)(2,1)S(1)}, u32[]{:S(2)}, u32[]{:S(2)}) collective-permute-start(bf16[56,128]{1,0:T(8,128)(2,1)S(1)} %get-tuple-element.36), channel_id=1, source_target_pairs={{0,1},{1,0},{2,3},{3,2},{4,5},{5,4},{6,7},{7,6},{8,9},{9,8},{10,11... | collective-permute-start | bytes 43016 | tf_op jit(solution)/shard_map/ppermute | solution.py:393
  31.4 5.9 %collective-permute-start.13 = (bf16[56,128]{1,0:T(8,128)(2,1)S(1)}, bf16[56,128]{1,0:T(8,128)(2,1)S(1)}, u32[]{:S(2)}, u32[]{:S(2)}) collective-permute-start(bf16[56,128]{1,0:T(8,128)(2,1)S(1)} %get-tuple-element.37), channel_id=1, source_target_pairs={{0,2},{1,3},{2,0},{3,1},{4,6},{5,7},{6,4},{7,5},{8,10},{9,11},{10,... | collective-permute-start | bytes 43016 | tf_op jit(solution)/shard_map/ppermute | solution.py:393
  32.7 4.5 %collective-permute-start.14 = (bf16[56,128]{1,0:T(8,128)(2,1)S(1)}, bf16[56,128]{1,0:T(8,128)(2,1)S(1)}, u32[]{:S(2)}, u32[]{:S(2)}) collective-permute-start(bf16[56,128]{1,0:T(8,128)(2,1)S(1)} %get-tuple-element.38), channel_id=1, source_target_pairs={{0,3},{1,2},{2,1},{3,0},{4,7},{5,6},{6,5},{7,4},{8,11},{9,10},{10,... | collective-permute-start | bytes 43016 | tf_op jit(solution)/shard_map/ppermute | solution.py:393

commit v4 on v3

--- a/solution.py
+++ b/solution.py
@@ -76,15 +76,10 @@
     kvw = kvq * HD
 
     def kernel(q_ref, ids_ref, blocks_ref, cache_ref, all_ref, live_ref, *rest):
-        q_out = rest[:SLAB]
-        kv_out = rest[SLAB : 2 * SLAB]
-        scratch, held, sem = rest[2 * SLAB :]
+        own_ref, near_ref, far_ref = rest[:3]
+        kv_out = rest[3 : 3 + SLAB]
+        (scratch,) = rest[3 + SLAB :]
         mine = lax.axis_index("seq") % SLAB
-        fetches = []
-        for p in range(prompts):
-            fetch = pltpu.make_async_copy(cache_ref.at[p], held.at[p], sem.at[p])
-            fetch.start()
-            fetches.append(fetch)
         for h in range(heads):
             scratch[pl.ds(h, cands, stride=heads), :] = q_ref[:, h * HD : (h + 1) * HD].astype(F32)
         all_ref[...] = scratch[...].astype(BF16)
@@ -99,33 +94,54 @@
                 for r in range(cands):
                     at = pl.multiple_of(r * heads + first + k * group, 8)
                     pieces.append(scratch[pl.ds(at, group), :])
-            q_out[j][...] = jnp.concatenate(pieces + id_rows, axis=0).astype(BF16)
-        for p in range(prompts):
-            fetches[p].wait()
-            for j in range(SLAB):
-                for side in range(2):
-                    column = pl.multiple_of(side * kv_width + (mine ^ j) * kvw, kvw)
-                    kv_out[j][side, p] = held[p, :, pl.ds(column, kvw)]
+            part = jnp.concatenate(pieces + id_rows, axis=0).astype(BF16)
+            if j < 2:
+                (own_ref, near_ref)[j][...] = part
+            else:
+                far_ref[(j - 2) * part_rows : (j - 1) * part_rows, :] = part
+        for j in range(SLAB):
+            for side in range(2):
+                column = pl.multiple_of(side * kv_width + (mine ^ j) * kvw, kvw)
+                kv_out[j][side] = cache_ref[:, :, pl.ds(column, kvw)]
 
     smem = pl.BlockSpec(memory_space=pltpu.SMEM)
     out = pl.pallas_call(
         kernel,
         out_shape=[pltpu.VMEM((cands * heads, HD), BF16), pltpu.VMEM((8, HD), jnp.int32)]
-        + [pltpu.VMEM((part_rows, HD), BF16)] * SLAB
+        + [pltpu.VMEM((rows, HD), BF16) for rows in (part_rows, part_rows, 2 * part_rows)]
         + [pltpu.VMEM((2, prompts, span, kvw), BF16)] * SLAB,
-        in_specs=[vmem_spec(), smem, smem, pl.BlockSpec(memory_space=pl.ANY)],
-        out_specs=[vmem_spec()] * (2 + 2 * SLAB),
+        in_specs=[vmem_spec(), smem, smem, vmem_spec()],
+        out_specs=[vmem_spec()] * (5 + SLAB),
         scratch_shapes=[
             pltpu.VMEM((cands * heads, HD), F32),
-            pltpu.VMEM((prompts, span, kv_width2), BF16),
-            pltpu.SemaphoreType.DMA((prompts,)),
         ],
         name="prepare",
     )(queries, prompt_of, blocks, prompt_cache)
-    return out[0], out[1], out[2 : 2 + SLAB], out[2 + SLAB :]
-
-
-def suffix_attend(live, rows_q, suffix_cache, kv_heads):
+    return out[0], out[1], out[2:5], out[5:]
+
+
+def pack(own, near_part, far, passed):
+    rows = own.shape[0]
+    half = rows - 8
+
+    def kernel(own_ref, near_ref, far_ref, passed_ref, out_ref):
+        segment = lax.broadcasted_iota(jnp.int32, (8, HD), 1) // (HD // SLAB)
+        ids = jnp.zeros((8, HD), F32)
+        for j, (ref, at) in enumerate(((own_ref, 0), (near_ref, 0), (far_ref, 0), (passed_ref, rows))):
+            out_ref[j * half : (j + 1) * half, :] = ref[at : at + half, :]
+            ids = jnp.where(segment == j, ref[at + half : at + rows, :].astype(F32), ids)
+        out_ref[SLAB * half :, :] = ids.astype(BF16)
+
+    return pl.pallas_call(
+        kernel,
+        out_shape=pltpu.VMEM((SLAB * half + 8, HD), BF16),
+        in_specs=[vmem_spec()] * 4,
+        out_specs=vmem_spec(),
+        name="pack",
+    )(*near([own, near_part, far, passed]))
+
+
+def suffix_attend(first, count, live, rows_q, suffix_cache, kv_heads):
     cands, length, kv_width2 = suffix_cache.shape
     kv_width = kv_width2 // 2
     heads = rows_q.shape[0] // cands
@@ -133,10 +149,10 @@
 
     def kernel(live_ref, q_ref, cache_ref, max_ref, sum_ref, mix_ref, keys, values, sem):
         fetches = []
-        for c in range(cands):
+        for c in range(count):
             for side, target in enumerate((keys, values)):
                 fetch = pltpu.make_async_copy(
-                    cache_ref.at[c, :, side * kv_width : (side + 1) * kv_width],
+                    cache_ref.at[first + c, :, side * kv_width : (side + 1) * kv_width],
                     target.at[c],
                     sem.at[c, side],
                 )
@@ -147,15 +163,18 @@
             == lax.broadcasted_iota(jnp.int32, (heads, kv_width), 1) // HD
         )
         position = lax.broadcasted_iota(jnp.int32, (heads, length), 1)
-        for c in range(cands):
+        for c in range(count):
             rows = slice(c * heads, (c + 1) * heads)
-            wide = jnp.concatenate([q_ref[rows, :]] * kv_heads, axis=1)
+            held = first * heads
+            wide = jnp.concatenate(
+                [q_ref[held + c * heads : held + (c + 1) * heads, :]] * kv_heads, axis=1
+            )
             wide = jnp.where(diagonal, wide, jnp.zeros_like(wide))
             fetches[2 * c].wait()
             logits = lax.dot_general(
                 wide, keys[c], (((1,), (1,)), ((), ())), preferred_element_type=F32
             ) * HD ** (-0.5)
-            live_row = jnp.concatenate([live_ref[c : c + 1, :]] * (length // HD), axis=1)
+            live_row = jnp.concatenate([live_ref[first + c : first + c + 1, :]] * (length // HD), axis=1)
             live = position < live_row
             logits = jnp.where(live, logits, floor_logit)
             maxima = jnp.max(logits, axis=1, keepdims=True)
@@ -173,18 +192,18 @@
 
     return pl.pallas_call(
         kernel,
-        out_shape=[pltpu.VMEM((cands * heads, HD), F32)] * 3,
+        out_shape=[pltpu.VMEM((count * heads, HD), F32)] * 3,
         in_specs=[vmem_spec(), vmem_spec(), pl.BlockSpec(memory_space=pl.ANY)],
         out_specs=[vmem_spec()] * 3,
         scratch_shapes=[
-            pltpu.VMEM((cands, length, kv_width), BF16),
-            pltpu.VMEM((cands, length, kv_width), BF16),
-            pltpu.SemaphoreType.DMA((cands, 2)),
+            pltpu.VMEM((count, length, kv_width), BF16),
+            pltpu.VMEM((count, length, kv_width), BF16),
+            pltpu.SemaphoreType.DMA((count, 2)),
         ],
         cost_estimate=pl.CostEstimate(
-            flops=4 * cands * heads * length * kv_width,
-            transcendentals=cands * heads * length,
-            bytes_accessed=2 * suffix_cache.size,
+            flops=4 * count * heads * length * kv_width,
+            transcendentals=count * heads * length,
+            bytes_accessed=2 * suffix_cache.size * count // cands,
         ),
         name="suffix",
     )(*near([live, rows_q]), suffix_cache)
@@ -195,7 +214,7 @@
     outer = query_blocks.shape[0] if stacked else len(query_blocks)
     chunk = math.gcd(outer, 4)
     part = cands * group
-    part_rows = kvq * part + 8
+    part_rows = kvq * part
     block_rows = SLAB * part
     out_rows = kvq * block_rows + stat_rows(kvq)
     prompts, _ = caches[0].shape[1:3]
@@ -211,11 +230,13 @@
             out_refs = refs[chunk + SLAB :]
         rows = [q_ref[...].astype(F32) for q_ref in q_refs]
         ids = []
+        segment = lax.broadcasted_iota(jnp.int32, (8, HD), 1) // (HD // SLAB)
         for i in range(chunk):
             for j in range(SLAB):
+                mine = jnp.where(segment == j, rows[i][SLAB * part_rows :], 0.0)
+                mine = jnp.max(mine, axis=1, keepdims=True)
                 for r in range(cands):
-                    at = j * part_rows + kvq * part + r
-                    ids.append(jnp.broadcast_to(rows[i][at : at + 1], (group, HD)))
+                    ids.append(jnp.broadcast_to(mine[r : r + 1], (group, HD)))
         ids = jnp.concatenate(ids, axis=0)
         picked = [ids == float(p) for p in range(prompts)]
         stats = [[] for _ in range(chunk)]
@@ -266,7 +287,7 @@
             kernel,
             out_shape=jax.ShapeDtypeStruct((outer, out_rows, HD), BF16),
             grid=(outer // chunk,),
-            in_specs=[pl.BlockSpec((chunk, SLAB * part_rows, HD), lambda s: (s, 0, 0))] + whole,
+            in_specs=[pl.BlockSpec((chunk, SLAB * part_rows + 8, HD), lambda s: (s, 0, 0))] + whole,
             out_specs=pl.BlockSpec((chunk, out_rows, HD), lambda s: (s, 0, 0)),
             name="prompt",
         )(query_blocks, *caches)
@@ -334,20 +355,25 @@
 
     def kernel(*refs):
         piece_refs = refs[:SLAB]
-        max_ref, sum_ref, mix_ref, reward_ref, out_ref, score_ref, scratch = refs[SLAB:]
+        state_refs = refs[SLAB : SLAB + len(suffix_state)]
+        reward_ref, out_ref, score_ref, scratch = refs[SLAB + len(suffix_state) :]
+        split = suffix_state[0].shape[0] // heads
         mine = lax.axis_index("seq") % SLAB
         scores = [jnp.zeros((group, HD), F32) for _ in range(cands)]
         for j in range(SLAB):
             first = (mine ^ j) * hq
-            stats = piece_refs[j][kvq * part :, :].astype(F32)
-            mix = piece_refs[j][: kvq * part, :].astype(F32)
+            piece = piece_refs[j][...].astype(F32)
+            mix, stats = piece[: kvq * part], piece[kvq * part :]
             for k in range(kvq):
                 maximum, total = unpack_stats(stats, k)
                 maximum = to_rows(maximum, part, j * part)
                 total = to_rows(total, part, j * part)
                 weight = reward_ref[pl.ds(pl.multiple_of(first + k * group, 8), group), :]
                 for r in range(cands):
-                    at = pl.ds(pl.multiple_of(r * heads + first + k * group, 8), group)
+                    base = r * heads if r < split else (r - split) * heads
+                    max_ref, sum_ref, mix_ref = state_refs[:3] if r < split else state_refs[3:]
+                    row = pl.ds(pl.multiple_of(r * heads + first + k * group, 8), group)
+                    at = pl.ds(pl.multiple_of(base + first + k * group, 8), group)
                     cut = slice(r * group, (r + 1) * group)
                     home_max = max_ref[at, :]
                     here_max = jnp.broadcast_to(maximum[cut], (group, HD))
@@ -357,7 +383,7 @@
                     total_all = home * sum_ref[at, :] + here * total[cut]
                     mixed = home * mix_ref[at, :] + here * mix[k * part :][cut]
                     attended = (mixed / total_all).astype(BF16).astype(F32)
-                    scratch[at, :] = attended
+                    scratch[row, :] = attended
                     scores[r] = scores[r] + attended * weight
         for h in range(heads):
             out_ref[:, h * HD : (h + 1) * HD] = scratch[pl.ds(h, cands, stride=heads), :].astype(
@@ -373,7 +399,7 @@
             jax.ShapeDtypeStruct((cands, heads * HD), BF16),
             jax.ShapeDtypeStruct((cands,), F32),
         ],
-        in_specs=[vmem_spec()] * (SLAB + 4),
+        in_specs=[vmem_spec()] * (SLAB + len(suffix_state) + 1),
         out_specs=[vmem_spec(), smem],
         scratch_shapes=[pltpu.VMEM((cands * heads, HD), F32)],
         name="finish",
@@ -395,16 +421,23 @@
     def spread(arrays, step):
         return [arrays[0]] + [hop(arrays[i], step * i) for i in range(1, len(arrays))]
 
+    def relay(own, near_part, far_part):
+        far = hop(far_part, 2)
+        return [own, hop(near_part, 1), far, hop(far, 1)]
+
     direct = is_direct(devices)
     columns = [[SLAB * z + i for z in range(outer)] for i in range(SLAB)]
 
     rows_q, live, q_parts, kv_parts = prepare(
         queries, prompt_of[:, 0], suffix_blocks, prompt_cache, kvq, group
     )
-    q_parts = spread(q_parts, 1)
     kv_parts = spread(kv_parts, 1)
-    q_slab = jnp.concatenate(q_parts, axis=0)
-    suffix_state = suffix_attend(live, rows_q, suffix_cache, kv_heads)
+    own, near_q, far_q, passed_q = relay(*q_parts)
+    q_slab = pack(own, near_q, far_q, passed_q)
+    early = (2 * cands + 2) // 3
+    suffix_state = []
+    for first, count in ((0, early), (early, cands - early)):
+        suffix_state += suffix_attend(first, count, live, rows_q, suffix_cache, kv_heads)
     if direct:
         q_all = spread([q_slab] * outer, SLAB)
     else:

time: 38.4 us -> 48 us (1.25)
  waiting for transfers between devices: 12.3 us -> 17.9 us
  starting transfers between devices: 16.8 us -> 20.3 us
  Pallas kernels: 8.24 us -> 8.84 us
    ppermute x15, waiting for transfers between devices: 12.3 us -> 17.9 us  [hop(): return lax.ppermute(x, 'seq', [(i, i ^ step) for i in range(devices)])]
    ppermute x15, starting transfers between devices: 16.8 us -> 20.3 us  [hop(): return lax.ppermute(x, 'seq', [(i, i ^ step) for i in range(devices)])]
    pallas_call x1 -> x3, Pallas kernels: 4.02 us -> 5.25 us  [the longest x2 5.24 us: suffix_attend(): pl.pallas_call(kernel, out_shape=[pltpu.VMEM((count * heads, HD), F32)] *...]
    pallas_call x1, Pallas kernels: 2.15 us -> 1.49 us  [prepare(): pl.pallas_call(kernel, out_shape=[pltpu.VMEM((cands * heads, HD), BF16),...]
  transfers between devices with their start and end apart: 15 -> 15, of which waited for: 7 -> 6; matrix products, arithmetic and copies ran while one was open for 0% -> 0% of each run, Pallas kernels for 11% -> 11%
where the time goes in v4:
time: 48 us; the launch traced here: 47.8 us
  starting transfers between devices  20.3 us (42%)
  waiting for transfers between devices  17.9 us (37%)
  Pallas kernels  8.84 us (18%)
  between operations  0.73 us (2%)
    ppermute x15, starting transfers between devices, hop(): return lax.ppermute(x, 'seq', [(i, i ^ step) for i in range(devices)])  20.3 us
    ppermute x15, waiting for transfers between devices, hop(): return lax.ppermute(x, 'seq', [(i, i ^ step) for i in range(devices)])  17.9 us
    pallas_call x2, Pallas kernels, suffix_attend(): pl.pallas_call(kernel, out_shape=[pltpu.VMEM((count * heads, HD), F32)] *...  5.24 us
    pallas_call x1, Pallas kernels, prepare(): pl.pallas_call(kernel, out_shape=[pltpu.VMEM((cands * heads, HD), BF16),...  1.49 us
    pallas_call x1, Pallas kernels, prompt_attend(): pl.pallas_call(kernel, out_shape=[pltpu.VMEM((out_rows, HD), BF16)] * out...  1.03 us
  transfers between devices with their start and end apart: 15, of which 6 were waited for; matrix products, arithmetic and copies ran while one was open for 0% of the time, Pallas kernels for 11%

profile of v4, /device:TPU:0, one launch (start us, length us, event | category | flops | bytes accessed | tf_op | source)
XLA Modules:
  0.0 47.8 jit_solution(1151751027767353582)
XLA Ops:
  0.6 1.5 %prepare.1 = (bf16[192,128]{1,0:T(8,128)(2,1)S(1)}, s32[8,128]{1,0:T(8,128)S(1)}, bf16[56,128]{1,0:T(8,128)(2,1)S(1)}, bf16[56,128]{1,0:T(8,128)(2,1)S(1)}, bf16...) custom-call(bf16[3,8192]{1,0:T(4,128)(2,1)} %q_ref.1, ...), custom_call_target="tpu_custom_call" | custom-call | tf_op jit(solution)/shard_map/prepare/pallas_call | solution.py:108
  2.1 0.6 %collective-permute-start.6 = (bf16[2,2,128,256]{3,2,1,0:T(8,128)(2,1)S(1)}, bf16[2,2,128,256]{3,2,1,0:T(8,128)(2,1)S(1)}, u32[]{:S(2)}, u32[]{:S(2)}) collective-permute-start(bf16[2,2,128,256]{3,2,1,0:T(8,128)(2,1)S(1)} %get-tuple-element.29), channel_id=1, source_target_pairs={{0,1},{1,0},{2,3},{3,2},{4,5},{5,4},{6,7},{7,6},{8,9},{9,8},{10,11... | collective-permute-start | bytes 786440 | tf_op jit(solution)/shard_map/ppermute | solution.py:419
  2.7 2.6 %collective-permute-start.7 = (bf16[2,2,128,256]{3,2,1,0:T(8,128)(2,1)S(1)}, bf16[2,2,128,256]{3,2,1,0:T(8,128)(2,1)S(1)}, u32[]{:S(2)}, u32[]{:S(2)}) collective-permute-start(bf16[2,2,128,256]{3,2,1,0:T(8,128)(2,1)S(1)} %get-tuple-element.30), channel_id=1, source_target_pairs={{0,2},{1,3},{2,0},{3,1},{4,6},{5,7},{6,4},{7,5},{8,10},{9,11},{10,... | collective-permute-start | bytes 786440 | tf_op jit(solution)/shard_map/ppermute | solution.py:419
  5.3 0.0 collective-permute-start.8
  5.3 1.7 %collective-permute-start.1 = (bf16[112,128]{1,0:T(8,128)(2,1)S(1)}, bf16[112,128]{1,0:T(8,128)(2,1)S(1)}, u32[]{:S(2)}, u32[]{:S(2)}) collective-permute-start(bf16[112,128]{1,0:T(8,128)(2,1)S(1)} %get-tuple-element.27), channel_id=1, source_target_pairs={{0,2},{1,3},{2,0},{3,1},{4,6},{5,7},{6,4},{7,5},{8,10},{9,11},{10,... | collective-permute-start | bytes 86024 | tf_op jit(solution)/shard_map/ppermute | solution.py:419
  7.1 11.3 %collective-permute-done.1.far_ref = bf16[112,128]{1,0:T(8,128)(2,1)S(1)} collective-permute-done((bf16[112,128]{1,0:T(8,128)(2,1)S(1)}, bf16[112,128]{1,0:T(8,128)(2,1)S(1)}, u32[]{:S(2)}, u32[]{:S(2)}) %collective-permute-start.1) | collective-permute-done | bytes 28704 | tf_op jit(solution)/shard_map/ppermute | solution.py:419
  18.4 0.0 collective-permute-start.2
  18.4 0.5 %collective-permute-start = (bf16[56,128]{1,0:T(8,128)(2,1)S(1)}, bf16[56,128]{1,0:T(8,128)(2,1)S(1)}, u32[]{:S(2)}, u32[]{:S(2)}) collective-permute-start(bf16[56,128]{1,0:T(8,128)(2,1)S(1)} %get-tuple-element.26), channel_id=1, source_target_pairs={{0,1},{1,0},{2,3},{3,2},{4,5},{5,4},{6,7},{7,6},{8,9},{9,8},{10,11... | collective-permute-start | bytes 43016 | tf_op jit(solution)/shard_map/ppermute | solution.py:419
  18.9 0.8 %collective-permute-done.near_ref = bf16[56,128]{1,0:T(8,128)(2,1)S(1)} collective-permute-done((bf16[56,128]{1,0:T(8,128)(2,1)S(1)}, bf16[56,128]{1,0:T(8,128)(2,1)S(1)}, u32[]{:S(2)}, u32[]{:S(2)}) %collective-permute-start) | collective-permute-done | bytes 14368 | tf_op jit(solution)/shard_map/ppermute | solution.py:419
  19.7 0.0 collective-permute-done.2.passed_ref
  19.8 1.9 %collective-permute-start.3 = (bf16[200,128]{1,0:T(8,128)(2,1)S(1)}, bf16[200,128]{1,0:T(8,128)(2,1)S(1)}, u32[]{:S(2)}, u32[]{:S(2)}) collective-permute-start(bf16[200,128]{1,0:T(8,128)(2,1)S(1)} %pack.1.refs_0_), channel_id=1, source_target_pairs={{0,4},{1,5},{2,6},{3,7},{4,0},{5,1},{6,2},{7,3},{8,12},{9,13},{10,... | collective-permute-start | bytes 153608 | tf_op jit(solution)/shard_map/ppermute | solution.py:419
  21.6 2.6 %collective-permute-start.4 = (bf16[200,128]{1,0:T(8,128)(2,1)S(1)}, bf16[200,128]{1,0:T(8,128)(2,1)S(1)}, u32[]{:S(2)}, u32[]{:S(2)}) collective-permute-start(bf16[200,128]{1,0:T(8,128)(2,1)S(1)} %pack.1.refs_0_), channel_id=1, source_target_pairs={{0,8},{1,9},{2,10},{3,11},{4,12},{5,13},{6,14},{7,15},{8,0},{9,1},... | collective-permute-start | bytes 153608 | tf_op jit(solution)/shard_map/ppermute | solution.py:419
  24.2 0.0 collective-permute-done.3.refs_1_
  24.2 4.1 %collective-permute-start.5 = (bf16[200,128]{1,0:T(8,128)(2,1)S(1)}, bf16[200,128]{1,0:T(8,128)(2,1)S(1)}, u32[]{:S(2)}, u32[]{:S(2)}) collective-permute-start(bf16[200,128]{1,0:T(8,128)(2,1)S(1)} %pack.1.refs_0_), channel_id=1, source_target_pairs={{0,12},{1,13},{2,14},{3,15},{4,8},{5,9},{6,10},{7,11},{8,4},{9,5},... | collective-permute-start | bytes 153608 | tf_op jit(solution)/shard_map/ppermute | solution.py:419
  28.3 0.0 collective-permute-done.4.refs_2_
  28.3 2.1 %collective-permute-done.5.refs_3_ = bf16[200,128]{1,0:T(8,128)(2,1)S(1)} collective-permute-done((bf16[200,128]{1,0:T(8,128)(2,1)S(1)}, bf16[200,128]{1,0:T(8,128)(2,1)S(1)}, u32[]{:S(2)}, u32[]{:S(2)}) %collective-permute-start.5) | collective-permute-done | bytes 51232 | tf_op jit(solution)/shard_map/ppermute | solution.py:419
  30.4 0.0 collective-permute-done.6.refs_5_
  30.4 0.0 collective-permute-done.7.refs_6_
  30.4 0.0 collective-permute-done.8.refs_7_
  30.4 1.0 %prompt.1 = (bf16[200,128]{1,0:T(8,128)(2,1)S(1)}, bf16[200,128]{1,0:T(8,128)(2,1)S(1)}, bf16[200,128]{1,0:T(8,128)(2,1)S(1)}, bf16[200,128]{1,0:T(8,128)(2,1)S(1)}) custom-call(bf16[200,128]{1,0:T(8,128)(2,1)S(1)} %pack.1.refs_0_, bf16[200,128]{1,0:T(8,128)(2,1)S(1)} %collective-permute-done.3.refs_1_, bf16[200,128]{1,0:T(8,128)(2,1)S(1)} %collective-permute-done.4.refs_2_, ...), custom_call_target="tpu_custom_call" | custom-call | tf_op jit(solution)/shard_map/prompt/pallas_call | solution.py:294
  31.5 1.2 %collective-permute-start.10 = (bf16[200,128]{1,0:T(8,128)(2,1)S(1)}, bf16[200,128]{1,0:T(8,128)(2,1)S(1)}, u32[]{:S(2)}, u32[]{:S(2)}) collective-permute-start(bf16[200,128]{1,0:T(8,128)(2,1)S(1)} %get-tuple-element.34), channel_id=1, source_target_pairs={{0,8},{1,9},{2,10},{3,11},{4,12},{5,13},{6,14},{7,15},{8,0},{9,1},... | collective-permute-start | bytes 153608 | tf_op jit(solution)/shard_map/ppermute | solution.py:419
  32.7 2.8 %collective-permute-start.11 = (bf16[200,128]{1,0:T(8,128)(2,1)S(1)}, bf16[200,128]{1,0:T(8,128)(2,1)S(1)}, u32[]{:S(2)}, u32[]{:S(2)}) collective-permute-start(bf16[200,128]{1,0:T(8,128)(2,1)S(1)} %get-tuple-element.35), channel_id=1, source_target_pairs={{0,12},{1,13},{2,14},{3,15},{4,8},{5,9},{6,10},{7,11},{8,4},{9,5},... | collective-permute-start | bytes 153608 | tf_op jit(solution)/shard_map/ppermute | solution.py:419
  35.4 0.5 %collective-permute-start.9 = (bf16[200,128]{1,0:T(8,128)(2,1)S(1)}, bf16[200,128]{1,0:T(8,128)(2,1)S(1)}, u32[]{:S(2)}, u32[]{:S(2)}) collective-permute-start(bf16[200,128]{1,0:T(8,128)(2,1)S(1)} %get-tuple-element.33), channel_id=1, source_target_pairs={{0,4},{1,5},{2,6},{3,7},{4,0},{5,1},{6,2},{7,3},{8,12},{9,13},{10,... | collective-permute-start | bytes 153608 | tf_op jit(solution)/shard_map/ppermute | solution.py:419
  35.9 0.7 %collective-permute-done.10.refs_2_ = bf16[200,128]{1,0:T(8,128)(2,1)S(1)} collective-permute-done((bf16[200,128]{1,0:T(8,128)(2,1)S(1)}, bf16[200,128]{1,0:T(8,128)(2,1)S(1)}, u32[]{:S(2)}, u32[]{:S(2)}) %collective-permute-start.10) | collective-permute-done | bytes 51232 | tf_op jit(solution)/shard_map/ppermute | solution.py:419
  36.6 2.0 %collective-permute-done.11.refs_3_ = bf16[200,128]{1,0:T(8,128)(2,1)S(1)} collective-permute-done((bf16[200,128]{1,0:T(8,128)(2,1)S(1)}, bf16[200,128]{1,0:T(8,128)(2,1)S(1)}, u32[]{:S(2)}, u32[]{:S(2)}) %collective-permute-start.11) | collective-permute-done | bytes 51232 | tf_op jit(solution)/shard_map/ppermute | solution.py:419
  38.6 1.0 %collective-permute-done.9.refs_1_ = bf16[200,128]{1,0:T(8,128)(2,1)S(1)} collective-permute-done((bf16[200,128]{1,0:T(8,128)(2,1)S(1)}, bf16[200,128]{1,0:T(8,128)(2,1)S(1)}, u32[]{:S(2)}, u32[]{:S(2)}) %collective-permute-start.9) | collective-permute-done | bytes 51232 | tf_op jit(solution)/shard_map/ppermute | solution.py:419
  39.5 0.2 merge.1
  39.7 0.1 collective-permute-start.12
  39.8 1.6 %collective-permute-start.13 = (bf16[56,128]{1,0:T(8,128)(2,1)S(1)}, bf16[56,128]{1,0:T(8,128)(2,1)S(1)}, u32[]{:S(2)}, u32[]{:S(2)}) collective-permute-start(bf16[56,128]{1,0:T(8,128)(2,1)S(1)} %get-tuple-element.38), channel_id=1, source_target_pairs={{0,2},{1,3},{2,0},{3,1},{4,6},{5,7},{6,4},{7,5},{8,10},{9,11},{10,... | collective-permute-start | bytes 43016 | tf_op jit(solution)/shard_map/ppermute | solution.py:419
  41.4 0.3 collective-permute-start.14
  41.7 0.0 copy-start
  41.7 3.1 %suffix.2 = (f32[128,128]{1,0:T(8,128)S(1)}, f32[128,128]{1,0:T(8,128)S(1)}, f32[128,128]{1,0:T(8,128)S(1)}) custom-call(s32[8,128]{1,0:T(8,128)S(1)} %get-tuple-element.40.live_ref, bf16[192,128]{1,0:T(8,128)(2,1)S(1)} %get-tuple-element.41.q_ref, bf16[3,512,2048]{2,1,0:T(8,128)(2,1)} %cache_ref.5), custom_call_target="tpu_custom_call" | custom-call | flops 268435456 | bytes 4194304 | tf_op jit(solution)/shard_map/suffix/pallas_call | solution.py:193
  44.8 2.2 %suffix.3 = (f32[64,128]{1,0:T(8,128)S(1)}, f32[64,128]{1,0:T(8,128)S(1)}, f32[64,128]{1,0:T(8,128)S(1)}) custom-call(s32[8,128]{1,0:T(8,128)S(1)} %get-tuple-element.40.live_ref, bf16[192,128]{1,0:T(8,128)(2,1)S(1)} %get-tuple-element.41.q_ref, bf16[3,512,2048]{2,1,0:T(8,128)(2,1)} %cache_ref.5), custom_call_target="tpu_custom_call" | custom-call | flops 134217728 | bytes 2097152 | tf_op jit(solution)/shard_map/suffix/pallas_call | solution.py:193
  46.9 0.0 collective-permute-done.12.refs_1_
  46.9 0.0 collective-permute-done.13.refs_2_
  46.9 0.0 collective-permute-done.14.refs_3_
  47.0 0.0 copy-done
  47.0 0.9 %finish.1 = (bf16[3,8192]{1,0:T(4,128)(2,1)}, f32[3]{0:T(128)}) custom-call(bf16[56,128]{1,0:T(8,128)(2,1)S(1)} %get-tuple-element.36.refs_0_, bf16[56,128]{1,0:T(8,128)(2,1)S(1)} %collective-permute-done.12.refs_1_, bf16[56,128]{1,0:T(8,128)(2,1)S(1)} %collective-permute-done.13.refs_2_, bf16[56,128]{1,0:T(8,128)(2,1)S(1)} %collective-permute-done.14.refs_3_, ...), custom_call_target="tpu_custom_call" | custom-call | tf_op jit(solution)/shard_map/finish/pallas_call | solution.py:396
  (1 shorter events, 0.0 us)
Async XLA Ops:
  2.1 28.3 %collective-permute-start.6 = (bf16[2,2,128,256]{3,2,1,0:T(8,128)(2,1)S(1)}, bf16[2,2,128,256]{3,2,1,0:T(8,128)(2,1)S(1)}, u32[]{:S(2)}, u32[]{:S(2)}) collective-permute-start(bf16[2,2,128,256]{3,2,1,0:T(8,128)(2,1)S(1)} %get-tuple-element.29), channel_id=1, source_target_pairs={{0,1},{1,0},{2,3},{3,2},{4,5},{5,4},{6,7},{7,6},{8,9},{9,8},{10,11... | collective-permute-start | bytes 786440 | tf_op jit(solution)/shard_map/ppermute | solution.py:419
  2.7 27.7 %collective-permute-start.7 = (bf16[2,2,128,256]{3,2,1,0:T(8,128)(2,1)S(1)}, bf16[2,2,128,256]{3,2,1,0:T(8,128)(2,1)S(1)}, u32[]{:S(2)}, u32[]{:S(2)}) collective-permute-start(bf16[2,2,128,256]{3,2,1,0:T(8,128)(2,1)S(1)} %get-tuple-element.30), channel_id=1, source_target_pairs={{0,2},{1,3},{2,0},{3,1},{4,6},{5,7},{6,4},{7,5},{8,10},{9,11},{10,... | collective-permute-start | bytes 786440 | tf_op jit(solution)/shard_map/ppermute | solution.py:419
  5.3 25.1 %collective-permute-start.8 = (bf16[2,2,128,256]{3,2,1,0:T(8,128)(2,1)S(1)}, bf16[2,2,128,256]{3,2,1,0:T(8,128)(2,1)S(1)}, u32[]{:S(2)}, u32[]{:S(2)}) collective-permute-start(bf16[2,2,128,256]{3,2,1,0:T(8,128)(2,1)S(1)} %get-tuple-element.31), channel_id=1, source_target_pairs={{0,3},{1,2},{2,1},{3,0},{4,7},{5,6},{6,5},{7,4},{8,11},{9,10},{10,... | collective-permute-start | bytes 786440 | tf_op jit(solution)/shard_map/ppermute | solution.py:419
  5.3 13.1 %collective-permute-start.1 = (bf16[112,128]{1,0:T(8,128)(2,1)S(1)}, bf16[112,128]{1,0:T(8,128)(2,1)S(1)}, u32[]{:S(2)}, u32[]{:S(2)}) collective-permute-start(bf16[112,128]{1,0:T(8,128)(2,1)S(1)} %get-tuple-element.27), channel_id=1, source_target_pairs={{0,2},{1,3},{2,0},{3,1},{4,6},{5,7},{6,4},{7,5},{8,10},{9,11},{10,... | collective-permute-start | bytes 86024 | tf_op jit(solution)/shard_map/ppermute | solution.py:419
  18.4 1.4 %collective-permute-start.2 = (bf16[112,128]{1,0:T(8,128)(2,1)S(1)}, bf16[112,128]{1,0:T(8,128)(2,1)S(1)}, u32[]{:S(2)}, u32[]{:S(2)}) collective-permute-start(bf16[112,128]{1,0:T(8,128)(2,1)S(1)} %collective-permute-done.1.far_ref), channel_id=1, source_target_pairs={{0,1},{1,0},{2,3},{3,2},{4,5},{5,4},{6,7},{7,6},{8,9},{9,8},{10,11... | collective-permute-start | bytes 86024 | tf_op jit(solution)/shard_map/ppermute | solution.py:419
  18.4 1.3 %collective-permute-start = (bf16[56,128]{1,0:T(8,128)(2,1)S(1)}, bf16[56,128]{1,0:T(8,128)(2,1)S(1)}, u32[]{:S(2)}, u32[]{:S(2)}) collective-permute-start(bf16[56,128]{1,0:T(8,128)(2,1)S(1)} %get-tuple-element.26), channel_id=1, source_target_pairs={{0,1},{1,0},{2,3},{3,2},{4,5},{5,4},{6,7},{7,6},{8,9},{9,8},{10,11... | collective-permute-start | bytes 43016 | tf_op jit(solution)/shard_map/ppermute | solution.py:419
  19.8 4.5 %collective-permute-start.3 = (bf16[200,128]{1,0:T(8,128)(2,1)S(1)}, bf16[200,128]{1,0:T(8,128)(2,1)S(1)}, u32[]{:S(2)}, u32[]{:S(2)}) collective-permute-start(bf16[200,128]{1,0:T(8,128)(2,1)S(1)} %pack.1.refs_0_), channel_id=1, source_target_pairs={{0,4},{1,5},{2,6},{3,7},{4,0},{5,1},{6,2},{7,3},{8,12},{9,13},{10,... | collective-permute-start | bytes 153608 | tf_op jit(solution)/shard_map/ppermute | solution.py:419
  21.6 6.7 %collective-permute-start.4 = (bf16[200,128]{1,0:T(8,128)(2,1)S(1)}, bf16[200,128]{1,0:T(8,128)(2,1)S(1)}, u32[]{:S(2)}, u32[]{:S(2)}) collective-permute-start(bf16[200,128]{1,0:T(8,128)(2,1)S(1)} %pack.1.refs_0_), channel_id=1, source_target_pairs={{0,8},{1,9},{2,10},{3,11},{4,12},{5,13},{6,14},{7,15},{8,0},{9,1},... | collective-permute-start | bytes 153608 | tf_op jit(solution)/shard_map/ppermute | solution.py:419
  24.2 6.2 %collective-permute-start.5 = (bf16[200,128]{1,0:T(8,128)(2,1)S(1)}, bf16[200,128]{1,0:T(8,128)(2,1)S(1)}, u32[]{:S(2)}, u32[]{:S(2)}) collective-permute-start(bf16[200,128]{1,0:T(8,128)(2,1)S(1)} %pack.1.refs_0_), channel_id=1, source_target_pairs={{0,12},{1,13},{2,14},{3,15},{4,8},{5,9},{6,10},{7,11},{8,4},{9,5},... | collective-permute-start | bytes 153608 | tf_op jit(solution)/shard_map/ppermute | solution.py:419
  31.5 5.1 %collective-permute-start.10 = (bf16[200,128]{1,0:T(8,128)(2,1)S(1)}, bf16[200,128]{1,0:T(8,128)(2,1)S(1)}, u32[]{:S(2)}, u32[]{:S(2)}) collective-permute-start(bf16[200,128]{1,0:T(8,128)(2,1)S(1)} %get-tuple-element.34), channel_id=1, source_target_pairs={{0,8},{1,9},{2,10},{3,11},{4,12},{5,13},{6,14},{7,15},{8,0},{9,1},... | collective-permute-start | bytes 153608 | tf_op jit(solution)/shard_map/ppermute | solution.py:419
  32.7 5.9 %collective-permute-start.11 = (bf16[200,128]{1,0:T(8,128)(2,1)S(1)}, bf16[200,128]{1,0:T(8,128)(2,1)S(1)}, u32[]{:S(2)}, u32[]{:S(2)}) collective-permute-start(bf16[200,128]{1,0:T(8,128)(2,1)S(1)} %get-tuple-element.35), channel_id=1, source_target_pairs={{0,12},{1,13},{2,14},{3,15},{4,8},{5,9},{6,10},{7,11},{8,4},{9,5},... | collective-permute-start | bytes 153608 | tf_op jit(solution)/shard_map/ppermute | solution.py:419
  35.4 4.1 %collective-permute-start.9 = (bf16[200,128]{1,0:T(8,128)(2,1)S(1)}, bf16[200,128]{1,0:T(8,128)(2,1)S(1)}, u32[]{:S(2)}, u32[]{:S(2)}) collective-permute-start(bf16[200,128]{1,0:T(8,128)(2,1)S(1)} %get-tuple-element.33), channel_id=1, source_target_pairs={{0,4},{1,5},{2,6},{3,7},{4,0},{5,1},{6,2},{7,3},{8,12},{9,13},{10,... | collective-permute-start | bytes 153608 | tf_op jit(solution)/shard_map/ppermute | solution.py:419
  39.7 7.2 %collective-permute-start.12 = (bf16[56,128]{1,0:T(8,128)(2,1)S(1)}, bf16[56,128]{1,0:T(8,128)(2,1)S(1)}, u32[]{:S(2)}, u32[]{:S(2)}) collective-permute-start(bf16[56,128]{1,0:T(8,128)(2,1)S(1)} %get-tuple-element.37), channel_id=1, source_target_pairs={{0,1},{1,0},{2,3},{3,2},{4,5},{5,4},{6,7},{7,6},{8,9},{9,8},{10,11... | collective-permute-start | bytes 43016 | tf_op jit(solution)/shard_map/ppermute | solution.py:419
  39.8 7.1 %collective-permute-start.13 = (bf16[56,128]{1,0:T(8,128)(2,1)S(1)}, bf16[56,128]{1,0:T(8,128)(2,1)S(1)}, u32[]{:S(2)}, u32[]{:S(2)}) collective-permute-start(bf16[56,128]{1,0:T(8,128)(2,1)S(1)} %get-tuple-element.38), channel_id=1, source_target_pairs={{0,2},{1,3},{2,0},{3,1},{4,6},{5,7},{6,4},{7,5},{8,10},{9,11},{10,... | collective-permute-start | bytes 43016 | tf_op jit(solution)/shard_map/ppermute | solution.py:419
  41.4 5.5 %collective-permute-start.14 = (bf16[56,128]{1,0:T(8,128)(2,1)S(1)}, bf16[56,128]{1,0:T(8,128)(2,1)S(1)}, u32[]{:S(2)}, u32[]{:S(2)}) collective-permute-start(bf16[56,128]{1,0:T(8,128)(2,1)S(1)} %get-tuple-element.39), channel_id=1, source_target_pairs={{0,3},{1,2},{2,1},{3,0},{4,7},{5,6},{6,5},{7,4},{8,11},{9,10},{10,... | collective-permute-start | bytes 43016 | tf_op jit(solution)/shard_map/ppermute | solution.py:419
  41.7 5.3 %copy-start = (f32[8192]{0:T(1024)S(1)}, f32[8192]{0:T(1024)}, u32[]{:S(2)}) copy-start(f32[8192]{0:T(1024)} %param.11) | copy-start | bytes 98308
